TPU v7x, 512 devices: a whole 4x4x16 slice. The times are simulated.
512 devices in a mesh: frame: 16 (over z), dom: 8 (over x, core), coef: 4 (over y).
Axes of the slice: x: 4, y: 4, z: 16, core: 2. Of those that a mesh axis runs over, the one named last changes fastest.
Arguments:
- geometry: float32 [32, 524288], P('coef', ('frame', 'dom')), may hold values from -1 to 1
- fraction: float32 [32, 524288], P('coef', ('frame', 'dom')), may hold values from 0 to 1
- interval: int32 [32, 524288], P('coef', ('frame', 'dom')), may hold values from 0 to 156
- pattern: int32 [32, 4096], P('coef', ('frame', 'dom')), may hold values from 0 to 95
- target: float32 [524288], P(('frame', 'dom')), may hold values from -8 to 8
Outputs:
- solution: float32 [384, 160], P('coef')
- residual: float32 [524288], P(('frame', 'dom'))
Inputs may be any that keep to these rules, and one draw needn't show every extreme that they name: The spline of a slot reads coefficients interval to interval + 3 of its type. Slot s refers to pair type (s // 8) * 96 + pattern.
All inputs are finite; a program needn't handle non-finite values.
Results may differ from a plain program's by a relative error of at most 0.0003.
Values sent between devices are 32-bit elements; how exact they have to be, the bound alone decides.
No kernel may reach another device: no remote copies, remote signals or barrier semaphores. Data moves between devices by JAX's collectives and lax.ppermute only.
A program may use at most 64 MiB of HBM per device.

v0:
```python
import math

import jax
import jax.numpy as jnp
from jax import lax
from jax.sharding import PartitionSpec as P

NK = 160
TYPES = 384
ITERS = 2


def spline_weights(fraction):
    square = fraction * fraction
    cube = square * fraction
    return (
        (1.0 - fraction) ** 3 / 6.0,
        (3.0 * cube - 6.0 * square + 4.0) / 6.0,
        (-3.0 * cube + 3.0 * square + 3.0 * fraction + 1.0) / 6.0,
        cube / 6.0,
    )


def dense_tiles(geom, fraction, interval):
    knots = lax.broadcasted_iota(jnp.int32, (1, NK, 1), 1)
    tiles = jnp.zeros((geom.shape[0], NK, geom.shape[1]), jnp.float32)
    for offset, weight in enumerate(spline_weights(fraction)):
        hit = knots == (interval + offset)[:, None, :]
        tiles = tiles + jnp.where(hit, (geom * weight)[:, None, :], 0.0)
    return tiles


def block_layout(geom):
    tiles_all = geom.shape[1] // 128
    block = math.gcd(8, tiles_all)
    return (block, block * 128, tiles_all // block)


def block_tiles(geometry, fraction, interval, pattern, index, block, width):
    start = index * width
    geom = lax.dynamic_slice_in_dim(geometry, start, width, 1)
    frac = lax.dynamic_slice_in_dim(fraction, start, width, 1)
    knot = lax.dynamic_slice_in_dim(interval, start, width, 1)
    kinds = lax.dynamic_slice_in_dim(pattern, index * block, block, 1)
    tiles = dense_tiles(geom, frac, knot).reshape(geom.shape[0], NK, block, 128)
    return (tiles, kinds, start)


def forward(coeffs, geometry, fraction, interval, pattern):
    block, width, count = block_layout(geometry)

    def forward_step(index, image):
        tiles, kinds, start = block_tiles(
            geometry, fraction, interval, pattern, index, block, width
        )
        chosen = jnp.take(coeffs, kinds, axis=0)
        part = jnp.einsum("sktr,stk->tr", tiles, chosen, precision=lax.Precision.HIGHEST)
        return lax.dynamic_update_slice_in_dim(image, part.reshape(width), start, 0)

    return lax.fori_loop(0, count, forward_step, jnp.zeros((geometry.shape[1],), jnp.float32))


def backward(resid, per_coef, geometry, fraction, interval, pattern):
    block, width, count = block_layout(geometry)
    owners = lax.broadcasted_iota(jnp.int32, (1, 1, per_coef), 2)

    def backward_step(index, total):
        tiles, kinds, start = block_tiles(
            geometry, fraction, interval, pattern, index, block, width
        )
        piece = lax.dynamic_slice_in_dim(resid, start, width, 0).reshape(block, 128)
        contrib = jnp.einsum("sktr,tr->stk", tiles, piece, precision=lax.Precision.HIGHEST)
        picks = (kinds[:, :, None] == owners).astype(jnp.float32)
        return total + jnp.einsum("stc,stk->ck", picks, contrib, precision=lax.Precision.HIGHEST)

    return lax.fori_loop(0, count, backward_step, jnp.zeros((per_coef, NK), jnp.float32))


def on_device(geometry, fraction, interval, pattern, target):
    per_coef = TYPES // lax.axis_size("coef")

    def transpose_sum(resid):
        local = backward(resid, per_coef, geometry, fraction, interval, pattern).reshape(
            per_coef * NK
        )
        share = lax.psum(local, ("frame", "dom"))
        total = lax.psum(jnp.sum(share * share), "coef")
        return (share, total)

    def expand(share):
        return share.reshape(per_coef, NK)

    residual = target
    gradient, gamma = transpose_sum(residual)
    direction = gradient
    solution = jnp.zeros_like(gradient)
    for step_index in range(ITERS):
        partial_image = forward(expand(direction), geometry, fraction, interval, pattern)
        image = lax.psum(partial_image, "coef")
        image_total = lax.psum(jnp.sum(image * image), ("frame", "dom"))
        alpha = gamma / image_total
        solution = solution + alpha * direction
        residual = residual - alpha * image
        if step_index + 1 < ITERS:
            gradient, gamma_next = transpose_sum(residual)
            direction = gradient + gamma_next / gamma * direction
            gamma = gamma_next
    return (expand(solution), residual)


def solution(mesh):
    in_specs = (
        P("coef", ("frame", "dom")),
        P("coef", ("frame", "dom")),
        P("coef", ("frame", "dom")),
        P("coef", ("frame", "dom")),
        P(("frame", "dom")),
    )
    out_specs = (P("coef", None), P(("frame", "dom")))
    return jax.shard_map(
        on_device, mesh=mesh, in_specs=in_specs, out_specs=out_specs, check_vma=False
    )
```

profile of v0, /device:TPU:1, one launch (start us, length us, event | category | flops | bytes accessed | tf_op | source)
XLA Modules:
  0.0 1750.1 jit_solution(9884929640221820795)
XLA Ops:
  0.6 52.4 %while.56 = (s32[]{:T(128)}, f32[96,160]{0,1:T(8,128)S(1)}, s32[8,32]{1,0:T(8,128)}, f32[4096]{0:T(1024)}, s32[8,4096]{1,0:T(8,128)}, /*index=5*/f32[8,4096]{1,0...) while((s32[]{:T(128)}, f32[96,160]{0,1:T(8,128)S(1)}, ...), condition=%wide.region_1.2_spmd.clone, body=%wide.region_0.1_spmd.clone.sunk | while | flops 42192900 | bytes 11854863 | solution.py:76
  0.7 0.8 fusion.117
  1.5 0.8 dynamic-slice_bitcast_fusion.10
  2.4 1.9 select_add_fusion.10
  5.0 8.4 fusion.118
  13.8 0.8 fusion.117
  14.6 0.8 dynamic-slice_bitcast_fusion.10
  15.5 1.9 select_add_fusion.10
  18.1 8.4 fusion.118
  26.9 0.8 fusion.117
  27.8 0.8 dynamic-slice_bitcast_fusion.10
  28.6 1.9 select_add_fusion.10
  31.2 8.4 fusion.118
  40.0 0.8 fusion.117
  41.7 1.9 select_add_fusion.10
  44.3 8.4 fusion.118
  53.3 498.0 %psum.56 = f32[15360]{0:T(1024)S(1)} all-reduce(f32[15360]{0:T(1024)S(1)} %reshape.226), channel_id=1, replica_groups=mesh['frame'=16,'dom'=8,'coef'=4] {'frame','dom'}, use_global_device_ids=true, to_apply=%region_2.3 | all-reduce | flops 15360 | bytes 122880 | tf_op jit(solution)/shard_map/psum | solution.py:86
  551.4 53.3 %while.54 = (s32[]{:T(128)}, f32[4096]{0:T(1024)S(1)}, s32[8,4096]{1,0:T(8,128)}, f32[8,4096]{1,0:T(8,128)}, f32[8,4096]{1,0:T(8,128)}, /*index=5*/s32[8,32]{1,0...) while((s32[]{:T(128)}, f32[4096]{0:T(1024)S(1)}, ...), condition=%wide.region_6.0_spmd, body=%wide.region_5.7_spmd.sunk | while | flops 30371208 | bytes 11859845 | solution.py:60
  551.5 0.8 fusion.106
  552.3 0.8 dynamic-slice_bitcast_fusion.8
  553.2 4.2 select_add_fusion.8
  558.3 6.1 fusion.108
  564.8 0.8 fusion.106
  565.6 0.8 dynamic-slice_bitcast_fusion.8
  566.5 4.2 select_add_fusion.8
  571.6 6.1 fusion.108
  578.1 0.8 fusion.106
  579.8 4.2 select_add_fusion.8
  585.0 6.1 fusion.108
  591.4 0.8 fusion.106
  593.1 4.2 select_add_fusion.8
  598.3 6.1 fusion.108
  605.3 14.6 all-reduce
  620.5 256.4 %psum.59 = f32[]{:T(128)} all-reduce(f32[]{:T(128)} %multiply_reduce_fusion.3), channel_id=1, replica_groups=mesh['frame'=16,'dom'=8,'coef'=4] {'frame','dom'}, use_global_device_ids=true, to_apply=%region_9.11 | all-reduce | flops 1 | bytes 8 | tf_op jit(solution)/shard_map/psum | solution.py:100
  878.3 49.7 %while.57 = (s32[]{:T(128)}, f32[96,160]{0,1:T(8,128)S(1)}, s32[8,32]{1,0:T(8,128)}, f32[4096]{0:T(1024)S(1)}, s32[8,4096]{1,0:T(8,128)}, /*index=5*/f32[8,4096]...) while((s32[]{:T(128)}, f32[96,160]{0,1:T(8,128)S(1)}, ...), condition=%wide.region_11.13_spmd.clone, body=%wide.region_10.12_spmd.clone.sunk | while | flops 42192900 | bytes 11854863 | solution.py:76
  878.3 0.8 fusion.123
  880.1 1.9 select_add_fusion.11
  882.0 8.4 fusion.124
  890.8 0.8 fusion.123
  892.5 1.9 select_add_fusion.11
  894.4 8.4 fusion.124
  903.2 0.8 fusion.123
  904.9 1.9 select_add_fusion.11
  906.9 8.4 fusion.124
  915.6 0.8 fusion.123
  917.3 1.9 select_add_fusion.11
  919.3 8.4 fusion.124
  928.3 485.9 %psum.60 = f32[15360]{0:T(1024)S(1)} all-reduce(f32[15360]{0:T(1024)S(1)} %reshape.228), channel_id=1, replica_groups=mesh['frame'=16,'dom'=8,'coef'=4] {'frame','dom'}, use_global_device_ids=true, to_apply=%region_12.14 | all-reduce | flops 15360 | bytes 122880 | tf_op jit(solution)/shard_map/psum | solution.py:86
  1414.8 6.9 psum.61
  1423.1 53.3 %while.55 = (s32[]{:T(128)}, f32[4096]{0:T(1024)S(1)}, s32[8,4096]{1,0:T(8,128)}, f32[8,4096]{1,0:T(8,128)}, f32[8,4096]{1,0:T(8,128)}, /*index=5*/s32[8,32]{1,0...) while((s32[]{:T(128)}, f32[4096]{0:T(1024)S(1)}, ...), condition=%wide.region_16.18_spmd, body=%wide.region_15.17_spmd.sunk | while | flops 30371208 | bytes 11859845 | solution.py:60
  1423.1 0.8 fusion.111
  1424.8 4.2 select_add_fusion.9
  1430.0 6.1 fusion.113
  1436.4 0.8 fusion.111
  1438.2 4.2 select_add_fusion.9
  1443.3 6.1 fusion.113
  1449.8 0.8 fusion.111
  1451.5 4.2 select_add_fusion.9
  1456.6 6.1 fusion.113
  1463.1 0.8 fusion.111
  1464.8 4.2 select_add_fusion.9
  1470.0 6.1 fusion.113
  1476.4 12.1 psum.62
  1489.1 258.2 %psum.63 = f32[]{:T(128)} all-reduce(f32[]{:T(128)} %multiply_reduce_fusion.2), channel_id=1, replica_groups=mesh['frame'=16,'dom'=8,'coef'=4] {'frame','dom'}, use_global_device_ids=true, to_apply=%region_19.21 | all-reduce | flops 1 | bytes 8 | tf_op jit(solution)/shard_map/psum | solution.py:100
  (265 shorter events, 29.5 us)
Async XLA Ops:
  4.3 9.1 copy-start
  17.4 9.1 copy-start
  30.5 9.1 copy-start
  43.6 9.1 copy-start
  551.4 326.9 %copy-start.4 = (f32[4096]{0:T(1024)S(1)}, f32[4096]{0:T(1024)}, u32[]{:S(2)}) copy-start(f32[4096]{0:T(1024)} %get-tuple-element.1094) | copy-start | bytes 49156
  551.4 6.0 copy-start.1
  564.8 6.0 copy-start.1
  578.1 6.0 copy-start.1
  591.4 6.0 copy-start.1
  882.0 8.4 copy-start.2
  894.4 8.4 copy-start.2
  906.8 8.4 copy-start.2
  919.3 8.4 copy-start.2
  1423.1 6.0 copy-start.3
  1436.4 6.0 copy-start.3
  1449.8 6.0 copy-start.3
  1463.1 6.0 copy-start.3
where the time goes:
time: 1750 us
  blocking collectives  1530 us (87%)
  matrix products  118 us (7%)
  other arithmetic  78.9 us (5%)
    psum x2, blocking collectives, transpose_sum(): share = lax.psum(local, ('frame', 'dom'))  984 us
    psum x2, blocking collectives, on_device(): image_total = lax.psum(jnp.sum(image * image), ('frame', 'dom'))  515 us
    dot_general x8, matrix products, backward_step(): jnp.einsum('sktr,tr->stk', tiles, piece, precision=lax.Precision.HIGHEST)  66.9 us
    add x16, other arithmetic, dense_tiles(): tiles = tiles + jnp.where(hit, (geom * weight)[:, None, :], 0.0)  49.2 us
    dot_general x8, matrix products, forward_step(): jnp.einsum('sktr,stk->tr', tiles, chosen, precision=lax.Precision.HIGHEST)  49 us

commit v1 on v0

v1 whole, which is shorter than its diff:
```python
import functools

import jax
import jax.numpy as jnp
from jax import lax
from jax.experimental import pallas as pl
from jax.experimental.pallas import tpu as pltpu
from jax.sharding import PartitionSpec as P

NK = 160
TYPES = 384
TD = 96
HIGH = 24
KNOTS = TD + HIGH
TABLE = 128
PAIRS = 256
IMAGE = 40

VMEM = pl.BlockSpec(memory_space=pltpu.VMEM)
F32 = jnp.float32
BF16 = jnp.bfloat16


def call(kernel, name, *shapes):
    outs = [jax.ShapeDtypeStruct(s, F32) for s in shapes]
    return functools.partial(_run, kernel, name, outs)


def _run(kernel, name, outs, *args, scratch=()):
    return pl.pallas_call(
        kernel,
        out_shape=outs,
        in_specs=[VMEM] * len(args),
        out_specs=[VMEM] * len(outs),
        scratch_shapes=list(scratch),
        name=name,
    )(*args)


def split(value):
    high = value.astype(BF16)
    return high, (value - high.astype(F32)).astype(BF16)


def total_of(value):
    return jnp.sum(jnp.sum(value, axis=0, keepdims=True), axis=1, keepdims=True)


def parts_sum(ref, count, rows):
    total = ref[0:rows, :]
    for at in range(1, count):
        total = total + ref[at * rows : (at + 1) * rows, :]
    return total


def weights(u):
    square = u * u
    cube = square * u
    rest = 1.0 - u
    return (
        rest * rest * rest * (1.0 / 6.0),
        (3.0 * cube - 6.0 * square + 4.0) * (1.0 / 6.0),
        (-3.0 * cube + 3.0 * square + 3.0 * u + 1.0) * (1.0 / 6.0),
        cube * (1.0 / 6.0),
    )


POWERS = (
    (1.0 / 6.0, -0.5, 0.5, -1.0 / 6.0),
    (2.0 / 3.0, 0.0, -1.0, 0.5),
    (1.0 / 6.0, 0.5, 0.5, -0.5),
    (0.0, 0.0, 0.0, 1.0 / 6.0),
)


def power_rows(first):
    sub = lax.broadcasted_iota(jnp.int32, (8, 128), 0)
    out = []
    for power in range(4):
        row = jnp.zeros((8, 128), F32)
        for j in range(4):
            if POWERS[j][power]:
                row = jnp.where(sub == first + j, POWERS[j][power], row)
        out.append(row)
    return out


def transposed(geom_ref, frac_ref, knot_ref, patt_ref, resid_ref, total, out_ref, parts_ref, tops_ref, tile_count):
    knots = lax.broadcasted_iota(jnp.int32, (NK // 16, 16, 128), 0) * 16 + lax.broadcasted_iota(
        jnp.int32, (NK // 16, 16, 128), 1
    )
    knots = knots.astype(F32).astype(BF16)
    one, zero = jnp.ones((), BF16), jnp.zeros((), BF16)
    powers = (power_rows(0), power_rows(4))

    def tile(t, _):
        lanes = pl.ds(pl.multiple_of(t * 128, 128), 128)
        amount = geom_ref[:, lanes] * resid_ref[pl.ds(t, 1), :]
        frac = frac_ref[:, lanes]
        knot = knot_ref[:, lanes].astype(F32)
        for pair in range(4):
            values, hits = [], []
            for half in range(2):
                s = 2 * pair + half
                p0, p1, p2, p3 = powers[half]
                u = jnp.broadcast_to(frac[s : s + 1, :], (8, 128))
                a = jnp.broadcast_to(amount[s : s + 1, :], (8, 128))
                values.append(a * (p0 + u * (p1 + u * (p2 + u * p3))))
                at = jnp.broadcast_to(knot[s : s + 1, :], (16, 128)).astype(BF16)
                hits.append(jnp.where(knots == at[None], one, zero).reshape(NK, 128))
            value = jnp.concatenate(values, axis=1)
            rounded = value.astype(BF16).astype(F32)
            left = jnp.concatenate([rounded, value - rounded], axis=0).astype(BF16)
            got = lax.dot_general(
                left, jnp.concatenate(hits, axis=1), (((1,), (1,)), ((), ())), preferred_element_type=F32
            )
            rows = pl.ds(pl.multiple_of((t * 4 + pair) * 8, 8), 8)
            got = got[0:8, :] + got[8:16, :]
            parts_ref[rows, :] = got[:, 0:128]
            tops_ref[rows, 0 : NK - 128] = got[:, 128:NK]
        return 0

    tops_ref[...] = jnp.zeros((4 * PAIRS, 128), F32)
    lax.fori_loop(0, tile_count, tile, 0)

    lane = lax.broadcasted_iota(jnp.int32, (8, 128), 1)
    picks = jnp.concatenate(
        [jnp.where(lane == patt_ref[:, t : t + 1], 1.0, 0.0) for t in range(tile_count)], axis=0
    )
    picks = jnp.transpose(picks).astype(BF16)[0:TD, :]
    grad = None
    for j in range(4):
        rows = pl.ds(j, PAIRS, stride=4)
        piece = jnp.concatenate([parts_ref[rows, :], tops_ref[rows, :]], axis=1)
        high, low = split(piece)
        got = jnp.dot(picks, high, preferred_element_type=F32) + jnp.dot(picks, low, preferred_element_type=F32)
        grad = got if j == 0 else grad + pltpu.roll(got, j, 1)
    out_ref[0:TD, :] = grad[:, 0:128]
    top = grad[:, 128:256]
    packed = top[0:HIGH]
    for q in range(1, 4):
        packed = packed + pltpu.roll(top[q * HIGH : (q + 1) * HIGH], 32 * q, 1)
    out_ref[TD:KNOTS, :] = packed
    sub = lax.broadcasted_iota(jnp.int32, (8, 128), 0)
    out_ref[KNOTS:TABLE, :] = jnp.where(sub == 0, total, 0.0)


def applied(geom_ref, frac_ref, knot_ref, patt_ref, table, out_ref, chosen_ref, tile_count):
    lane = lax.broadcasted_iota(jnp.int32, (8, 128), 1)
    low_rows, high_rows, shifts = [], [], []
    for t in range(tile_count):
        kind = jnp.broadcast_to(patt_ref[:, t : t + 1], (8, 128))
        block = jnp.where(kind >= HIGH, 1, 0) + jnp.where(kind >= 2 * HIGH, 1, 0) + jnp.where(kind >= 3 * HIGH, 1, 0)
        low_rows.append(jnp.where(lane == kind, 1.0, 0.0))
        high_rows.append(jnp.where(lane == TD + kind - HIGH * block, 1.0, 0.0))
        shifts.append(32 * block)
    picks = jnp.concatenate(low_rows + high_rows, axis=0).astype(BF16)
    high, low = split(table)
    chosen_ref[...] = jnp.dot(picks, high, preferred_element_type=F32) + jnp.dot(
        picks, low, preferred_element_type=F32
    )
    for t in range(tile_count):
        lanes = slice(128 * t, 128 * (t + 1))
        base = knot_ref[:, lanes]
        first = chosen_ref[8 * t : 8 * t + 8, :]
        last = chosen_ref[PAIRS + 8 * t : PAIRS + 8 * t + 8, :]
        value = None
        for j, weight in enumerate(weights(frac_ref[:, lanes])):
            at = base + j
            near = jnp.take_along_axis(first, at & 127, axis=1, mode="promise_in_bounds")
            far = jnp.take_along_axis(last, (at & 31) + shifts[t], axis=1, mode="promise_in_bounds")
            term = weight * jnp.where(at >= 128, far, near)
            value = term if j == 0 else value + term
        row = jnp.sum(geom_ref[:, lanes] * value, axis=0, keepdims=True)
        for c in range(out_ref.shape[0] // IMAGE):
            out_ref[c * IMAGE + t : c * IMAGE + t + 1, :] = row
    gamma = jnp.broadcast_to(total_of(table[0:KNOTS] * table[0:KNOTS]), (8, 128))
    for c in range(out_ref.shape[0] // IMAGE):
        out_ref[c * IMAGE + 32 : (c + 1) * IMAGE, :] = gamma


def first_back(geom, frac, knot, patt, resid, out, parts, tops):
    transposed(geom, frac, knot, patt, resid, 0.0, out, parts, tops, 32)


def later_back(geom, frac, knot, patt, got, out, image, gamma, parts, tops):
    whole = parts_sum(got, got.shape[0] // IMAGE, IMAGE)
    image[...] = whole[0:32]
    gamma[...] = whole[32:40]
    total = jnp.broadcast_to(total_of(whole[0:32] * whole[0:32]), (8, 128))
    transposed(geom, frac, knot, patt, image, total, out, parts, tops, 32)


def scattered(count, copies, got, out):
    rows = got.shape[0] // count
    total = parts_sum(got, count, rows)
    for at in range(copies):
        out[at * rows : (at + 1) * rows, :] = total


def first_forward(geom, frac, knot, patt, grad, out, chosen):
    applied(geom, frac, knot, patt, grad[...], out, chosen, 32)


def later_forward(geom, frac, knot, patt, grad, other, gamma, out, table, chosen):
    alpha = gamma[0:1, :] / other[KNOTS : KNOTS + 1, :]
    table[...] = grad[...] - alpha * other[...]
    applied(geom, frac, knot, patt, table[...], out, chosen, 32)


def norm_kernel(got, gamma, image, out, image_out, gamma_out):
    whole = parts_sum(got, got.shape[0] // IMAGE, IMAGE)
    gamma_out[...] = whole[32:40]
    beta = whole[32:33] / gamma[0:1, :]
    result = whole[0:32] + beta * image[...]
    image_out[...] = result
    out[...] = jnp.broadcast_to(total_of(result * result), out.shape)


def last_kernel(got, gamma0, gamma1, grad0, other, grad1, image0, image1, target, sol, resid):
    total1 = jnp.sum(got[...], axis=0, keepdims=True)
    alpha0 = gamma0[0:1, :] / other[KNOTS : KNOTS + 1, :]
    alpha1 = gamma1[0:1, :] / total1
    beta = gamma1[0:1, :] / gamma0[0:1, :]
    resid[...] = target[...] - alpha0 * image0[...] - alpha1 * image1[...]
    table = alpha0 * grad0[...] + alpha1 * (grad1[...] + beta * grad0[...])
    sol[:, 0:128] = table[0:TD]
    packed = table[TD:KNOTS]
    for q in range(4):
        piece = packed if q == 0 else pltpu.roll(packed, 128 - 32 * q, 1)
        sol[q * HIGH : (q + 1) * HIGH, 128:NK] = piece[:, 0:32]


def exchange(value, axis, count):
    rows = value.shape[0]
    got = lax.all_to_all(value.reshape(count, rows * 128 // count), axis, 0, 0, tiled=True)
    return got.reshape(rows, 128)


def on_device(geometry, fraction, interval, pattern, target):
    frames, doms, coefs = lax.axis_size("frame"), lax.axis_size("dom"), lax.axis_size("coef")
    data = (geometry, fraction, interval, pattern)
    target = target.reshape(32, 128)
    piece = TABLE // doms
    parts = [pltpu.VMEM((4 * PAIRS, 128), F32)] * 2
    chosen = [pltpu.VMEM((2 * PAIRS, 128), F32)]

    def reduced(local):
        got = exchange(local, "dom", doms)
        (mine,) = call(functools.partial(scattered, doms, frames), "scatter_dom", (frames * piece, 128))(got)
        got = exchange(mine, "frame", frames)
        (mine,) = call(functools.partial(scattered, frames, doms), "scatter_frame", (TABLE, 128))(got)
        return exchange(mine, "dom", doms)

    (local,) = call(first_back, "back0", (TABLE, 128))(*data, target, scratch=parts)
    grad0 = reduced(local)
    (local,) = call(first_forward, "fwd0", (coefs * IMAGE, 128))(*data, grad0, scratch=chosen)
    got = exchange(local, "coef", coefs)
    local, image0, gamma0 = call(later_back, "back1", (TABLE, 128), (32, 128), (8, 128))(*data, got, scratch=parts)
    other = reduced(local)
    local, grad1 = call(later_forward, "fwd1", (coefs * IMAGE, 128), (TABLE, 128))(
        *data, grad0, other, gamma0, scratch=chosen
    )
    got = exchange(local, "coef", coefs)
    local, image1, gamma1 = call(norm_kernel, "norm", (frames * doms, 128), (32, 128), (8, 128))(got, gamma0, image0)
    got = exchange(local, ("frame", "dom"), frames * doms)
    sol, resid = call(last_kernel, "last", (TD, NK), (32, 128))(
        got, gamma0, gamma1, grad0, other, grad1, image0, image1, target
    )
    return sol, resid.reshape(4096)


def solution(mesh):
    in_specs = (
        P("coef", ("frame", "dom")),
        P("coef", ("frame", "dom")),
        P("coef", ("frame", "dom")),
        P("coef", ("frame", "dom")),
        P(("frame", "dom")),
    )
    out_specs = (P("coef", None), P(("frame", "dom")))
    return jax.shard_map(on_device, mesh=mesh, in_specs=in_specs, out_specs=out_specs, check_vma=False)
```

time: 1750 us -> 166 us (0.09)
  blocking collectives: 1530 us -> 130 us
  matrix products: 118 us -> 0 us
  other arithmetic: 78.9 us -> 0 us
  Pallas kernels: 0 us -> 32.8 us
    psum x7 -> x0, blocking collectives: 1530 us -> none  [the longest x2 984 us: transpose_sum(): share = lax.psum(local, ('frame', 'dom'))]
    all_to_all x0 -> x9, blocking collectives: none -> 130 us  [exchange(): lax.all_to_all(value.reshape(count, rows * 128 // count), axis, 0, 0, til...]
    dot_general x24 -> x0, matrix products: 118 us -> none  [the longest x8 66.9 us: backward_step(): jnp.einsum('sktr,tr->stk', tiles, piece, precision=lax.Precision.HIGHEST)]
    add x18 -> x0, other arithmetic: 49.2 us -> none  [the longest x16 49.2 us: dense_tiles(): tiles = tiles + jnp.where(hit, (geom * weight)[:, None, :], 0.0)]
    pallas_call x0 -> x10, Pallas kernels: none -> 32.8 us  [_run(): pl.pallas_call(kernel, out_shape=outs, in_specs=[VMEM] * len(args), out_s...]
where the time goes in v1:
time: 166 us; the launch traced here: 165 us
  blocking collectives  130 us (78%)
  Pallas kernels  32.8 us (20%)
    all_to_all x9, blocking collectives, exchange(): lax.all_to_all(value.reshape(count, rows * 128 // count), axis, 0, 0, til...  130 us
    pallas_call x10, Pallas kernels, _run(): pl.pallas_call(kernel, out_shape=outs, in_specs=[VMEM] * len(args), out_s...  32.8 us

profile of v1, /device:TPU:1, one launch (start us, length us, event | category | flops | bytes accessed | tf_op | source)
XLA Modules:
  0.0 164.9 jit_solution(1983990532589178135)
XLA Ops:
  0.6 9.0 %back0.1 = f32[128,128]{1,0:T(8,128)} custom-call(f32[8,4096]{1,0:T(8,128)} %geom.7, f32[8,4096]{1,0:T(8,128)} %frac.7, s32[8,4096]{1,0:T(8,128)} %knot.7, s32[8,32]{1,0:T(8,128)} %patt.7, f32[32,128]{1,0:T(8,128)} %bitcast.43), custom_call_target="tpu_custom_call" | custom-call | tf_op jit(solution)/shard_map/back0/pallas_call | solution.py:30
  9.6 15.6 %all_to_all.83 = f32[8,1,2048]{2,1,0:T(1,128)} all-to-all(f32[8,1,2048]{2,1,0:T(1,128)} %bitcast.39), channel_id=1, replica_groups=mesh['frame'=16,'dom'=8,'coef'=4] {'dom'}, dimensions={0} | all-to-all | bytes 131072 | tf_op jit(solution)/shard_map/all_to_all | solution.py:236
  25.2 1.5 scatter_dom.2
  26.7 22.1 %all_to_all.84 = f32[16,1,2048]{2,1,0:T(1,128)} all-to-all(f32[16,1,2048]{2,1,0:T(1,128)} %bitcast.27), channel_id=1, replica_groups=mesh['frame'=16,'dom'=8,'coef'=4] {'frame'}, dimensions={0} | all-to-all | bytes 262144 | tf_op jit(solution)/shard_map/all_to_all | solution.py:236
  48.8 1.6 scatter_frame.2
  50.4 12.6 %all_to_all.85 = f32[8,1,2048]{2,1,0:T(1,128)} all-to-all(f32[8,1,2048]{2,1,0:T(1,128)} %bitcast.36), channel_id=1, replica_groups=mesh['frame'=16,'dom'=8,'coef'=4] {'dom'}, dimensions={0} | all-to-all | bytes 131072 | tf_op jit(solution)/shard_map/all_to_all | solution.py:236
  63.0 2.7 %fwd0.1 = f32[160,128]{1,0:T(8,128)} custom-call(f32[8,4096]{1,0:T(8,128)} %geom.7, f32[8,4096]{1,0:T(8,128)} %frac.7, s32[8,4096]{1,0:T(8,128)} %knot.7, s32[8,32]{1,0:T(8,128)} %patt.7, f32[128,128]{1,0:T(8,128)} %bitcast.22), custom_call_target="tpu_custom_call" | custom-call | tf_op jit(solution)/shard_map/fwd0/pallas_call | solution.py:30
  65.6 8.8 %all_to_all.86 = f32[4,1,5120]{2,1,0:T(1,128)} all-to-all(f32[4,1,5120]{2,1,0:T(1,128)} %bitcast.33), channel_id=1, replica_groups=mesh['frame'=16,'dom'=8,'coef'=4] {'coef'}, dimensions={0} | all-to-all | bytes 163840 | tf_op jit(solution)/shard_map/all_to_all | solution.py:236
  74.5 9.0 %back1.1 = (f32[128,128]{1,0:T(8,128)}, f32[32,128]{1,0:T(8,128)}, f32[8,128]{1,0:T(8,128)}) custom-call(f32[8,4096]{1,0:T(8,128)} %geom.7, f32[8,4096]{1,0:T(8,128)} %frac.7, s32[8,4096]{1,0:T(8,128)} %knot.7, s32[8,32]{1,0:T(8,128)} %patt.7, f32[160,128]{1,0:T(8,128)} %bitcast.32), custom_call_target="tpu_custom_call" | custom-call | tf_op jit(solution)/shard_map/back1/pallas_call | solution.py:30
  83.5 11.0 %all_to_all.87 = f32[8,1,2048]{2,1,0:T(1,128)} all-to-all(f32[8,1,2048]{2,1,0:T(1,128)} %bitcast.41), channel_id=1, replica_groups=mesh['frame'=16,'dom'=8,'coef'=4] {'dom'}, dimensions={0} | all-to-all | bytes 131072 | tf_op jit(solution)/shard_map/all_to_all | solution.py:236
  94.5 1.5 scatter_dom.3
  96.0 16.1 %all_to_all.88 = f32[16,1,2048]{2,1,0:T(1,128)} all-to-all(f32[16,1,2048]{2,1,0:T(1,128)} %bitcast.29), channel_id=1, replica_groups=mesh['frame'=16,'dom'=8,'coef'=4] {'frame'}, dimensions={0} | all-to-all | bytes 262144 | tf_op jit(solution)/shard_map/all_to_all | solution.py:236
  112.1 1.6 scatter_frame.3
  113.7 12.2 %all_to_all.89 = f32[8,1,2048]{2,1,0:T(1,128)} all-to-all(f32[8,1,2048]{2,1,0:T(1,128)} %bitcast.38), channel_id=1, replica_groups=mesh['frame'=16,'dom'=8,'coef'=4] {'dom'}, dimensions={0} | all-to-all | bytes 131072 | tf_op jit(solution)/shard_map/all_to_all | solution.py:236
  125.9 2.7 %fwd1.1 = (f32[160,128]{1,0:T(8,128)}, f32[128,128]{1,0:T(8,128)}) custom-call(f32[8,4096]{1,0:T(8,128)} %geom.7, f32[8,4096]{1,0:T(8,128)} %frac.7, s32[8,4096]{1,0:T(8,128)} %knot.7, s32[8,32]{1,0:T(8,128)} %patt.7, f32[128,128]{1,0:T(8,128)} %bitcast.23, f32[128,128]{1,0:T(8,128)} %bitcast.25, f32[8,128]{1,0:T(8,128)} %get-tuple-element.13.gamma.gamma0), custom_call_target="tpu_custom_call" | custom-call | tf_op jit(solution)/shard_map/fwd1/pallas_call | solution.py:30
  128.6 8.5 %all_to_all.90 = f32[4,1,5120]{2,1,0:T(1,128)} all-to-all(f32[4,1,5120]{2,1,0:T(1,128)} %bitcast.40), channel_id=1, replica_groups=mesh['frame'=16,'dom'=8,'coef'=4] {'coef'}, dimensions={0} | all-to-all | bytes 163840 | tf_op jit(solution)/shard_map/all_to_all | solution.py:236
  137.2 1.6 norm.1
  138.8 22.8 %all_to_all.91 = f32[128,1,128]{2,1,0:T(1,128)} all-to-all(f32[128,1,128]{2,1,0:T(1,128)} %bitcast.42), channel_id=1, replica_groups=mesh['frame'=16,'dom'=8,'coef'=4] {'frame','dom'}, dimensions={0} | all-to-all | bytes 131072 | tf_op jit(solution)/shard_map/all_to_all | solution.py:236
  161.6 1.7 %last.1 = (f32[96,160]{1,0:T(8,128)}, f32[32,128]{1,0:T(8,128)}) custom-call(f32[128,128]{1,0:T(8,128)} %bitcast.34, f32[8,128]{1,0:T(8,128)} %get-tuple-element.13.gamma.gamma0, f32[8,128]{1,0:T(8,128)} %get-tuple-element.17.gamma1, f32[128,128]{1,0:T(8,128)} %bitcast.24, f32[128,128]{1,0:T(8,128)} %bitcast.26, f32[128,128]{1,0:T(8,128)} %get-tuple-element.18.grad1, ...), custom_call_target="tpu_custom_call" | custom-call | tf_op jit(solution)/shard_map/last/pallas_call | solution.py:30
  163.3 1.6 copy.17

commit v2 on v1

--- a/solution.py
+++ b/solution.py
@@ -15,6 +15,7 @@
 TABLE = 128
 PAIRS = 256
 IMAGE = 40
+UNROLL = 4
 
 VMEM = pl.BlockSpec(memory_space=pltpu.VMEM)
 F32 = jnp.float32
@@ -34,6 +35,7 @@
         out_specs=[VMEM] * len(outs),
         scratch_shapes=list(scratch),
         name=name,
+        compiler_params=pltpu.CompilerParams(vmem_limit_bytes=8 << 20),
     )(*args)
 
 
@@ -93,20 +95,18 @@
     one, zero = jnp.ones((), BF16), jnp.zeros((), BF16)
     powers = (power_rows(0), power_rows(4))
 
-    def tile(t, _):
+    def tile(t):
         lanes = pl.ds(pl.multiple_of(t * 128, 128), 128)
-        amount = geom_ref[:, lanes] * resid_ref[pl.ds(t, 1), :]
-        frac = frac_ref[:, lanes]
-        knot = knot_ref[:, lanes].astype(F32)
+        resid = jnp.broadcast_to(resid_ref[pl.ds(t, 1), :], (8, 128))
         for pair in range(4):
             values, hits = [], []
             for half in range(2):
-                s = 2 * pair + half
+                s = slice(2 * pair + half, 2 * pair + half + 1)
                 p0, p1, p2, p3 = powers[half]
-                u = jnp.broadcast_to(frac[s : s + 1, :], (8, 128))
-                a = jnp.broadcast_to(amount[s : s + 1, :], (8, 128))
+                u = jnp.broadcast_to(frac_ref[s, lanes], (8, 128))
+                a = jnp.broadcast_to(geom_ref[s, lanes], (8, 128)) * resid
                 values.append(a * (p0 + u * (p1 + u * (p2 + u * p3))))
-                at = jnp.broadcast_to(knot[s : s + 1, :], (16, 128)).astype(BF16)
+                at = jnp.broadcast_to(knot_ref[s, lanes], (16, 128)).astype(F32).astype(BF16)
                 hits.append(jnp.where(knots == at[None], one, zero).reshape(NK, 128))
             value = jnp.concatenate(values, axis=1)
             rounded = value.astype(BF16).astype(F32)
@@ -118,10 +118,14 @@
             got = got[0:8, :] + got[8:16, :]
             parts_ref[rows, :] = got[:, 0:128]
             tops_ref[rows, 0 : NK - 128] = got[:, 128:NK]
+
+    def tiles(step, _):
+        for at in range(UNROLL):
+            tile(step * UNROLL + at)
         return 0
 
     tops_ref[...] = jnp.zeros((4 * PAIRS, 128), F32)
-    lax.fori_loop(0, tile_count, tile, 0)
+    lax.fori_loop(0, tile_count // UNROLL, tiles, 0)
 
     lane = lax.broadcasted_iota(jnp.int32, (8, 128), 1)
     picks = jnp.concatenate(
@@ -224,11 +228,14 @@
     beta = gamma1[0:1, :] / gamma0[0:1, :]
     resid[...] = target[...] - alpha0 * image0[...] - alpha1 * image1[...]
     table = alpha0 * grad0[...] + alpha1 * (grad1[...] + beta * grad0[...])
-    sol[:, 0:128] = table[0:TD]
-    packed = table[TD:KNOTS]
-    for q in range(4):
-        piece = packed if q == 0 else pltpu.roll(packed, 128 - 32 * q, 1)
-        sol[q * HIGH : (q + 1) * HIGH, 128:NK] = piece[:, 0:32]
+    turned = jnp.transpose(table)
+    sol[0:128, :] = turned[:, 0:TD]
+    lane = lax.broadcasted_iota(jnp.int32, (32, 128), 1)
+    top = pltpu.roll(turned[0:32], 128 - TD, 1)
+    for q in range(1, 4):
+        piece = pltpu.roll(turned[32 * q : 32 * q + 32], (128 - TD + HIGH * q) % 128, 1)
+        top = jnp.where(lane >= HIGH * q, piece, top)
+    sol[128:NK, :] = top[:, 0:TD]
 
 
 def exchange(value, axis, count):
@@ -264,10 +271,10 @@
     got = exchange(local, "coef", coefs)
     local, image1, gamma1 = call(norm_kernel, "norm", (frames * doms, 128), (32, 128), (8, 128))(got, gamma0, image0)
     got = exchange(local, ("frame", "dom"), frames * doms)
-    sol, resid = call(last_kernel, "last", (TD, NK), (32, 128))(
+    sol, resid = call(last_kernel, "last", (NK, TD), (32, 128))(
         got, gamma0, gamma1, grad0, other, grad1, image0, image1, target
     )
-    return sol, resid.reshape(4096)
+    return sol.T, resid.reshape(4096)
 
 
 def solution(mesh):

time: 166 us -> 139 us (0.84)
  Pallas kernels: 32.8 us -> 11.6 us
  blocking collectives: 130 us -> 122 us
  local copies, waits for them, and re-layouts: 1.63 us -> 4.13 us
    pallas_call x10, Pallas kernels: 32.8 us -> 11.6 us  [_run(): pl.pallas_call(kernel, out_shape=outs, in_specs=[VMEM] * len(args), out_s...]
    all_to_all x9, blocking collectives: 130 us -> 122 us  [exchange(): lax.all_to_all(value.reshape(count, rows * 128 // count), axis, 0, 0, til...]
    unnamed x1 -> x18, local copies, waits for them, and re-layouts: 1.63 us -> 4.13 us
where the time goes in v2:
time: 139 us; the launch traced here: 138 us
  blocking collectives  122 us (88%)
  Pallas kernels  11.6 us (8%)
  local copies, waits for them, and re-layouts  4.13 us (3%)
    all_to_all x9, blocking collectives, exchange(): lax.all_to_all(value.reshape(count, rows * 128 // count), axis, 0, 0, til...  122 us
    pallas_call x10, Pallas kernels, _run(): pl.pallas_call(kernel, out_shape=outs, in_specs=[VMEM] * len(args), out_s...  11.6 us
    unnamed x18, local copies, waits for them, and re-layouts  4.13 us

profile of v2, /device:TPU:1, one launch (start us, length us, event | category | flops | bytes accessed | tf_op | source)
XLA Modules:
  0.0 138.1 jit_solution(1877861076597933727)
XLA Ops:
  0.6 0.0 copy-start
  0.6 0.9 copy-done
  1.5 0.0 copy-start.2
  1.5 0.9 copy-done.2
  2.4 0.0 copy-start.4
  2.4 0.9 copy-done.4
  3.3 0.0 copy-start.5
  3.3 0.7 copy-done.5
  4.0 0.0 copy-start.7
  4.0 0.7 copy-done.7
  4.8 4.3 %back0.1 = f32[128,128]{1,0:T(8,128)S(1)} custom-call(f32[8,4096]{1,0:T(8,128)S(1)} %copy-done, f32[8,4096]{1,0:T(8,128)S(1)} %copy-done.2, s32[8,4096]{1,0:T(8,128)S(1)} %copy-done.4, s32[8,32]{1,0:T(8,128)S(1)} %copy-done.5, f32[32,128]{1,0:T(8,128)S(1)} %bitcast.44), custom_call_target="tpu_custom_call" | custom-call | tf_op jit(solution)/shard_map/back0/pallas_call | solution.py:31
  9.0 14.1 %all_to_all.83 = f32[8,1,2048]{2,1,0:T(1,128)S(1)} all-to-all(f32[8,1,2048]{2,1,0:T(1,128)S(1)} %bitcast.40), channel_id=1, replica_groups=mesh['frame'=16,'dom'=8,'coef'=4] {'dom'}, dimensions={0} | all-to-all | bytes 131072 | tf_op jit(solution)/shard_map/all_to_all | solution.py:243
  23.1 23.1 %all_to_all.84 = f32[16,1,2048]{2,1,0:T(1,128)S(1)} all-to-all(f32[16,1,2048]{2,1,0:T(1,128)S(1)} %bitcast.28), channel_id=1, replica_groups=mesh['frame'=16,'dom'=8,'coef'=4] {'frame'}, dimensions={0} | all-to-all | bytes 262144 | tf_op jit(solution)/shard_map/all_to_all | solution.py:243
  46.2 0.0 copy-start.1
  46.2 0.0 copy-start.3
  46.2 0.0 copy-start.6
  46.2 11.2 %all_to_all.85 = f32[8,1,2048]{2,1,0:T(1,128)S(1)} all-to-all(f32[8,1,2048]{2,1,0:T(1,128)S(1)} %bitcast.37), channel_id=1, replica_groups=mesh['frame'=16,'dom'=8,'coef'=4] {'dom'}, dimensions={0} | all-to-all | bytes 131072 | tf_op jit(solution)/shard_map/all_to_all | solution.py:243
  57.4 0.0 copy-done.1
  57.4 0.0 copy-done.3
  57.4 0.0 copy-done.6
  57.4 1.0 fwd0.1
  58.4 8.5 %all_to_all.86 = f32[4,1,5120]{2,1,0:T(1,128)S(1)} all-to-all(f32[4,1,5120]{2,1,0:T(1,128)S(1)} %bitcast.34), channel_id=1, replica_groups=mesh['frame'=16,'dom'=8,'coef'=4] {'coef'}, dimensions={0} | all-to-all | bytes 163840 | tf_op jit(solution)/shard_map/all_to_all | solution.py:243
  66.9 4.3 %back1.1 = (f32[128,128]{1,0:T(8,128)S(1)}, f32[32,128]{1,0:T(8,128)S(1)}, f32[8,128]{1,0:T(8,128)S(1)}) custom-call(f32[8,4096]{1,0:T(8,128)S(1)} %copy-done.1, f32[8,4096]{1,0:T(8,128)S(1)} %copy-done.3, s32[8,4096]{1,0:T(8,128)S(1)} %copy-done.4, s32[8,32]{1,0:T(8,128)S(1)} %copy-done.6, f32[160,128]{1,0:T(8,128)S(1)} %bitcast.33), custom_call_target="tpu_custom_call" | custom-call | tf_op jit(solution)/shard_map/back1/pallas_call | solution.py:31
  71.3 9.4 %all_to_all.87 = f32[8,1,2048]{2,1,0:T(1,128)S(1)} all-to-all(f32[8,1,2048]{2,1,0:T(1,128)S(1)} %bitcast.42), channel_id=1, replica_groups=mesh['frame'=16,'dom'=8,'coef'=4] {'dom'}, dimensions={0} | all-to-all | bytes 131072 | tf_op jit(solution)/shard_map/all_to_all | solution.py:243
  80.7 15.2 %all_to_all.88 = f32[16,1,2048]{2,1,0:T(1,128)S(1)} all-to-all(f32[16,1,2048]{2,1,0:T(1,128)S(1)} %bitcast.30), channel_id=1, replica_groups=mesh['frame'=16,'dom'=8,'coef'=4] {'frame'}, dimensions={0} | all-to-all | bytes 262144 | tf_op jit(solution)/shard_map/all_to_all | solution.py:243
  95.9 11.0 %all_to_all.89 = f32[8,1,2048]{2,1,0:T(1,128)S(1)} all-to-all(f32[8,1,2048]{2,1,0:T(1,128)S(1)} %bitcast.39), channel_id=1, replica_groups=mesh['frame'=16,'dom'=8,'coef'=4] {'dom'}, dimensions={0} | all-to-all | bytes 131072 | tf_op jit(solution)/shard_map/all_to_all | solution.py:243
  107.0 1.0 fwd1.1
  108.0 6.9 %all_to_all.90 = f32[4,1,5120]{2,1,0:T(1,128)S(1)} all-to-all(f32[4,1,5120]{2,1,0:T(1,128)S(1)} %bitcast.41), channel_id=1, replica_groups=mesh['frame'=16,'dom'=8,'coef'=4] {'coef'}, dimensions={0} | all-to-all | bytes 163840 | tf_op jit(solution)/shard_map/all_to_all | solution.py:243
  114.9 0.1 norm.1
  115.0 0.0 copy-start.8
  115.0 22.3 %all_to_all.91 = f32[128,1,128]{2,1,0:T(1,128)S(1)} all-to-all(f32[128,1,128]{2,1,0:T(1,128)S(1)} %bitcast.43), channel_id=1, replica_groups=mesh['frame'=16,'dom'=8,'coef'=4] {'frame','dom'}, dimensions={0} | all-to-all | bytes 131072 | tf_op jit(solution)/shard_map/all_to_all | solution.py:243
  137.3 0.0 copy-done.8
  137.3 0.8 last.1
  (4 shorter events, 0.1 us)
Async XLA Ops:
  0.6 0.9 copy-start
  1.5 0.9 copy-start.2
  2.4 0.9 copy-start.4
  3.3 0.7 copy-start.5
  4.0 0.7 copy-start.7
  46.2 11.2 %copy-start.1 = (f32[8,4096]{1,0:T(8,128)S(1)}, f32[8,4096]{1,0:T(8,128)}, u32[]{:S(2)}) copy-start(f32[8,4096]{1,0:T(8,128)} %geom.7) | copy-start | bytes 393220
  46.2 11.2 %copy-start.3 = (f32[8,4096]{1,0:T(8,128)S(1)}, f32[8,4096]{1,0:T(8,128)}, u32[]{:S(2)}) copy-start(f32[8,4096]{1,0:T(8,128)} %frac.7) | copy-start | bytes 393220
  46.2 11.2 %copy-start.6 = (s32[8,32]{1,0:T(8,128)S(1)}, s32[8,32]{1,0:T(8,128)}, u32[]{:S(2)}) copy-start(s32[8,32]{1,0:T(8,128)} %patt.7) | copy-start | bytes 3076
  115.0 22.3 %copy-start.8 = (f32[4096]{0:T(1024)S(1)}, f32[4096]{0:T(1024)}, u32[]{:S(2)}) copy-start(f32[4096]{0:T(1024)} %param.9) | copy-start | bytes 49156

commit v3 on v2

v3 whole, which is shorter than its diff:
```python
import functools

import jax
import jax.numpy as jnp
from jax import lax
from jax.experimental import pallas as pl
from jax.experimental.pallas import tpu as pltpu
from jax.sharding import PartitionSpec as P

NK = 160
TYPES = 384
TD = 96
HIGH = 24
KNOTS = TD + HIGH
TABLE = 128
PAIRS = 256
IMAGE = 40
UNROLL = 8
TILES_DEV = 32

VMEM = pl.BlockSpec(memory_space=pltpu.VMEM)
HBM = pl.BlockSpec(memory_space=pltpu.HBM)
F32 = jnp.float32
BF16 = jnp.bfloat16
I32 = jnp.int32


def call(kernel, name, outs, args, scratch=(), space=VMEM):
    outs = [o if isinstance(o, jax.ShapeDtypeStruct) else jax.ShapeDtypeStruct(o, F32) for o in outs]
    return pl.pallas_call(
        kernel,
        out_shape=outs,
        in_specs=[space] * len(args),
        out_specs=[VMEM] * len(outs),
        scratch_shapes=list(scratch),
        name=name,
        compiler_params=pltpu.CompilerParams(vmem_limit_bytes=8 << 20),
    )(*args)


def split(value):
    high = value.astype(BF16)
    return high, (value - high.astype(F32)).astype(BF16)


def total_of(value):
    return jnp.sum(jnp.sum(value, axis=0, keepdims=True), axis=1, keepdims=True)


def parts_sum(ref, count, rows):
    total = ref[0:rows, :]
    for at in range(1, count):
        total = total + ref[at * rows : (at + 1) * rows, :]
    return total


def weights(u):
    square = u * u
    cube = square * u
    rest = 1.0 - u
    return (
        rest * rest * rest * (1.0 / 6.0),
        (3.0 * cube - 6.0 * square + 4.0) * (1.0 / 6.0),
        (-3.0 * cube + 3.0 * square + 3.0 * u + 1.0) * (1.0 / 6.0),
        cube * (1.0 / 6.0),
    )


def prepare(frac_ref, knot_ref, patt_ref, place_ref, high_ref, picks_ref):
    knot = knot_ref[...]
    high = (knot * 205) >> 10
    place_ref[...] = (knot - 5 * high + 1).astype(F32) + frac_ref[...]
    high_ref[...] = high.astype(F32)
    lane = lax.broadcasted_iota(I32, (8, 128), 1)
    picks = [jnp.where(lane == patt_ref[:, t : t + 1], 1.0, 0.0) for t in range(TILES_DEV)]
    picks_ref[...] = jnp.transpose(jnp.concatenate(picks, axis=0))[0:TD, :].astype(BF16)


def transposed(geom_ref, place_ref, high_ref, picks_ref, resid_ref, total, out_ref, parts_ref):
    places = lax.broadcasted_iota(I32, (8, 128), 0).astype(F32)
    rows = lax.broadcasted_iota(I32, (2, 16, 128), 0) * 16 + lax.broadcasted_iota(I32, (2, 16, 128), 1)
    rows = rows.astype(F32).astype(BF16)
    one, zero = jnp.ones((), BF16), jnp.zeros((), BF16)
    empty = jnp.zeros((16, 128), BF16)

    def tile(t):
        lanes = pl.ds(pl.multiple_of(t * 128, 128), 128)
        resid = jnp.broadcast_to(resid_ref[pl.ds(t, 1), :], (8, 128)) * (1.0 / 6.0)
        for pair in range(4):
            values, hits = [], []
            for half in range(2):
                s = slice(2 * pair + half, 2 * pair + half + 1)
                near = jnp.abs(jnp.broadcast_to(place_ref[s, lanes], (8, 128)) - places)
                a = jnp.maximum(2.0 - near, 0.0)
                b = jnp.maximum(1.0 - near, 0.0)
                amount = jnp.broadcast_to(geom_ref[s, lanes], (8, 128)) * resid
                value = amount * (a * a * a - (4.0 * b) * (b * b))
                rounded = value.astype(BF16).astype(F32)
                values.append(jnp.concatenate([rounded, value - rounded], axis=0).astype(BF16))
                at = jnp.broadcast_to(high_ref[s, lanes], (16, 128)).astype(BF16)
                hits.append(jnp.where(rows == at[None], one, zero).reshape(32, 128))
            left = jnp.concatenate(
                [jnp.concatenate([values[0], empty], axis=1), jnp.concatenate([empty, values[1]], axis=1)], axis=0
            )
            got = lax.dot_general(
                left, jnp.concatenate(hits, axis=1), (((1,), (1,)), ((), ())), preferred_element_type=F32
            )
            at = pl.ds(pl.multiple_of((t * 4 + pair) * 16, 16), 16)
            parts_ref[at, 0:32] = jnp.concatenate([got[0:8] + got[8:16], got[16:24] + got[24:32]], axis=0)

    def tiles(step, _):
        for at in range(UNROLL):
            tile(step * UNROLL + at)
        return 0

    lax.fori_loop(0, TILES_DEV // UNROLL, tiles, 0)

    picks = picks_ref[...]
    block = lax.broadcasted_iota(I32, (PAIRS, 128), 1) >> 5
    halves = []
    for group in range(2):
        piece = parts_ref[pl.ds(4 * group, PAIRS, stride=8), :]
        for q in range(1, 4):
            other = pltpu.roll(parts_ref[pl.ds(4 * group + q, PAIRS, stride=8), :], 32 * q, 1)
            piece = jnp.where(block >= q, other, piece)
        halves.append(piece)
    high, low = split(jnp.concatenate(halves, axis=1))
    grad = jnp.dot(picks, high, preferred_element_type=F32) + jnp.dot(picks, low, preferred_element_type=F32)
    source = lax.broadcasted_iota(I32, (256, 256), 0)
    column = lax.broadcasted_iota(I32, (256, 256), 1)
    knot = jnp.where(column >= 128, 128 + (column & 31), column)
    spread = jnp.where(5 * (source & 31) + (source >> 5) == knot, 1.0, 0.0).astype(BF16)
    high, low = split(grad)
    grad = jnp.dot(high, spread, preferred_element_type=F32) + jnp.dot(low, spread, preferred_element_type=F32)
    out_ref[0:TD, :] = grad[:, 0:128]
    packed = grad[0:HIGH, 128:256]
    for q in range(1, 4):
        packed = jnp.where(block[0:HIGH] >= q, grad[q * HIGH : (q + 1) * HIGH, 128:256], packed)
    out_ref[TD:KNOTS, :] = packed
    sub = lax.broadcasted_iota(I32, (8, 128), 0)
    out_ref[KNOTS:TABLE, :] = jnp.where(sub == 0, total, 0.0)


def choose(patt_ref, picks_ref, shift_ref):
    lane = lax.broadcasted_iota(I32, (8, 128), 1)
    low_rows, high_rows = [], []
    for t in range(TILES_DEV):
        kind = jnp.broadcast_to(patt_ref[:, t : t + 1], (8, 128))
        block = jnp.where(kind >= HIGH, 1, 0) + jnp.where(kind >= 2 * HIGH, 1, 0) + jnp.where(kind >= 3 * HIGH, 1, 0)
        low_rows.append(jnp.where(lane == kind, 1.0, 0.0))
        high_rows.append(jnp.where(lane == TD + kind - HIGH * block, 1.0, 0.0))
        shift_ref[8 * t : 8 * t + 8, :] = 32 * block
    picks_ref[...] = jnp.concatenate(low_rows + high_rows, axis=0).astype(BF16)


def applied(geom_ref, frac_ref, knot_ref, picks_ref, shift_ref, table, out_ref, chosen_ref):
    picks = picks_ref[...]
    high, low = split(table)
    chosen_ref[...] = jnp.dot(picks, high, preferred_element_type=F32) + jnp.dot(
        picks, low, preferred_element_type=F32
    )
    for t in range(TILES_DEV):
        lanes = slice(128 * t, 128 * (t + 1))
        slots = slice(8 * t, 8 * t + 8)
        base = knot_ref[:, lanes]
        first = chosen_ref[slots, :]
        last = chosen_ref[PAIRS + 8 * t : PAIRS + 8 * t + 8, :]
        value = None
        for j, weight in enumerate(weights(frac_ref[:, lanes])):
            at = base + j
            near = jnp.take_along_axis(first, at & 127, axis=1, mode="promise_in_bounds")
            far = jnp.take_along_axis(last, (at & 31) + shift_ref[slots, :], axis=1, mode="promise_in_bounds")
            term = weight * jnp.where(at >= 128, far, near)
            value = term if j == 0 else value + term
        row = jnp.sum(geom_ref[:, lanes] * value, axis=0, keepdims=True)
        for c in range(out_ref.shape[0] // IMAGE):
            out_ref[c * IMAGE + t : c * IMAGE + t + 1, :] = row
    gamma = jnp.broadcast_to(total_of(table[0:KNOTS] * table[0:KNOTS]), (8, 128))
    for c in range(out_ref.shape[0] // IMAGE):
        out_ref[c * IMAGE + 32 : (c + 1) * IMAGE, :] = gamma


def first_back(*refs):
    sources, (out, *copies), (place, high, picks), (parts, sems) = refs[:5], refs[5:11], refs[11:14], refs[14:]
    moves = [pltpu.make_async_copy(a, b, sems.at[i]) for i, (a, b) in enumerate(zip(sources, copies, strict=True))]
    for move in moves:
        move.start()
    for move in moves:
        move.wait()
    geom, frac, knot, patt, target = copies
    prepare(frac, knot, patt, place, high, picks)
    transposed(geom, place, high, picks, target, 0.0, out, parts)


def later_back(geom, place, high, picks, got, out, image, gamma, parts):
    whole = parts_sum(got, got.shape[0] // IMAGE, IMAGE)
    image[...] = whole[0:32]
    gamma[...] = whole[32:40]
    total = jnp.broadcast_to(total_of(whole[0:32] * whole[0:32]), (8, 128))
    transposed(geom, place, high, picks, image, total, out, parts)


def scattered(count, copies, got, out):
    rows = got.shape[0] // count
    total = parts_sum(got, count, rows)
    for at in range(copies):
        out[at * rows : (at + 1) * rows, :] = total


def first_forward(geom, frac, knot, patt, grad, out, picks, shift, chosen):
    choose(patt, picks, shift)
    applied(geom, frac, knot, picks, shift, grad[...], out, chosen)


def later_forward(geom, frac, knot, picks, shift, grad, other, gamma, out, table, chosen):
    alpha = gamma[0:1, :] / other[KNOTS : KNOTS + 1, :]
    table[...] = grad[...] - alpha * other[...]
    applied(geom, frac, knot, picks, shift, table[...], out, chosen)


def norm_kernel(got, gamma, image, out, image_out, gamma_out):
    whole = parts_sum(got, got.shape[0] // IMAGE, IMAGE)
    gamma_out[...] = whole[32:40]
    beta = whole[32:33] / gamma[0:1, :]
    result = whole[0:32] + beta * image[...]
    image_out[...] = result
    out[...] = jnp.broadcast_to(total_of(result * result), out.shape)


def last_kernel(got, gamma0, gamma1, grad0, other, grad1, image0, image1, target, sol, resid):
    total1 = jnp.sum(got[...], axis=0, keepdims=True)
    alpha0 = gamma0[0:1, :] / other[KNOTS : KNOTS + 1, :]
    alpha1 = gamma1[0:1, :] / total1
    beta = gamma1[0:1, :] / gamma0[0:1, :]
    resid[...] = target[...] - alpha0 * image0[...] - alpha1 * image1[...]
    table = alpha0 * grad0[...] + alpha1 * (grad1[...] + beta * grad0[...])
    turned = jnp.transpose(table)
    sol[0:128, :] = turned[:, 0:TD]
    lane = lax.broadcasted_iota(I32, (32, 128), 1)
    top = pltpu.roll(turned[0:32], 128 - TD, 1)
    for q in range(1, 4):
        piece = pltpu.roll(turned[32 * q : 32 * q + 32], (128 - TD + HIGH * q) % 128, 1)
        top = jnp.where(lane >= HIGH * q, piece, top)
    sol[128:NK, :] = top[:, 0:TD]


def exchange(value, axis, count):
    rows = value.shape[0]
    got = lax.all_to_all(value.reshape(count, rows * 128 // count), axis, 0, 0, tiled=True)
    return got.reshape(rows, 128)


def on_device(geometry, fraction, interval, pattern, target):
    frames, doms, coefs = lax.axis_size("frame"), lax.axis_size("dom"), lax.axis_size("coef")
    piece = TABLE // doms
    shape = jax.ShapeDtypeStruct
    parts = pltpu.VMEM((8 * PAIRS, 128), F32)
    chosen = pltpu.VMEM((2 * PAIRS, 128), F32)

    def reduced(local):
        got = exchange(local, "dom", doms)
        (mine,) = call(functools.partial(scattered, doms, frames), "scatter_dom", [(frames * piece, 128)], [got])
        got = exchange(mine, "frame", frames)
        (mine,) = call(functools.partial(scattered, frames, doms), "scatter_frame", [(TABLE, 128)], [got])
        return exchange(mine, "dom", doms)

    sources = [geometry, fraction, interval, pattern, target.reshape(32, 128)]
    copies = [shape(s.shape, s.dtype) for s in sources]
    local, geom, frac, knot, patt, target, place, high, types = call(
        first_back,
        "back0",
        [(TABLE, 128), *copies, (8, 4096), (8, 4096), shape((TD, PAIRS), BF16)],
        sources,
        [parts, pltpu.SemaphoreType.DMA((5,))],
        HBM,
    )
    grad0 = reduced(local)
    local, picks, shift = call(
        first_forward,
        "fwd0",
        [(coefs * IMAGE, 128), shape((2 * PAIRS, 128), BF16), shape((PAIRS, 128), I32)],
        [geom, frac, knot, patt, grad0],
        [chosen],
    )
    got = exchange(local, "coef", coefs)
    local, image0, gamma0 = call(
        later_back, "back1", [(TABLE, 128), (32, 128), (8, 128)], [geom, place, high, types, got], [parts]
    )
    other = reduced(local)
    local, grad1 = call(
        later_forward,
        "fwd1",
        [(coefs * IMAGE, 128), (TABLE, 128)],
        [geom, frac, knot, picks, shift, grad0, other, gamma0],
        [chosen],
    )
    got = exchange(local, "coef", coefs)
    local, image1, gamma1 = call(
        norm_kernel, "norm", [(frames * doms, 128), (32, 128), (8, 128)], [got, gamma0, image0]
    )
    got = exchange(local, ("frame", "dom"), frames * doms)
    sol, resid = call(
        last_kernel,
        "last",
        [(NK, TD), (32, 128)],
        [got, gamma0, gamma1, grad0, other, grad1, image0, image1, target],
    )
    return sol.T, resid.reshape(4096)


def solution(mesh):
    in_specs = (
        P("coef", ("frame", "dom")),
        P("coef", ("frame", "dom")),
        P("coef", ("frame", "dom")),
        P("coef", ("frame", "dom")),
        P(("frame", "dom")),
    )
    out_specs = (P("coef", None), P(("frame", "dom")))
    return jax.shard_map(on_device, mesh=mesh, in_specs=in_specs, out_specs=out_specs, check_vma=False)
```

time: 139 us -> 135 us (0.971)
  Pallas kernels: 11.6 us -> 7.74 us
    pallas_call x10, Pallas kernels: 11.6 us -> 7.74 us  [call(): pl.pallas_call(kernel, out_shape=outs, in_specs=[space] * len(args), out_...]
    unnamed x18 -> x10, local copies, waits for them, and re-layouts: 4.13 us -> 4.11 us
where the time goes in v3:
time: 135 us; the launch traced here: 134 us
  blocking collectives  121 us (90%)
  Pallas kernels  7.74 us (6%)
  local copies, waits for them, and re-layouts  4.11 us (3%)
    all_to_all x9, blocking collectives, exchange(): lax.all_to_all(value.reshape(count, rows * 128 // count), axis, 0, 0, til...  121 us
    pallas_call x10, Pallas kernels, call(): pl.pallas_call(kernel, out_shape=outs, in_specs=[space] * len(args), out_...  7.74 us
    unnamed x10, local copies, waits for them, and re-layouts  4.11 us

profile of v3, /device:TPU:1, one launch (start us, length us, event | category | flops | bytes accessed | tf_op | source)
XLA Modules:
  0.0 134.0 jit_solution(7702618803153345271)
XLA Ops:
  0.6 0.0 copy-start
  0.6 0.9 copy-done
  1.5 0.0 copy-start.1
  1.5 0.9 copy-done.1
  2.4 0.0 copy-start.2
  2.4 0.9 copy-done.2
  3.3 0.0 copy-start.3
  3.3 0.7 copy-done.3
  4.1 0.0 copy-start.4
  4.1 0.7 copy-done.4
  4.8 2.7 %back0.1 = (f32[128,128]{1,0:T(8,128)S(1)}, f32[8,4096]{1,0:T(8,128)S(1)}, f32[8,4096]{1,0:T(8,128)S(1)}, s32[8,4096]{1,0:T(8,128)S(1)}, s32[8,32]{1,0:T(8,128)S...) custom-call(f32[8,4096]{1,0:T(8,128)S(1)} %copy-done, ...), custom_call_target="tpu_custom_call" | custom-call | tf_op jit(solution)/shard_map/back0/pallas_call | solution.py:30
  7.5 14.1 %all_to_all.83 = f32[8,1,2048]{2,1,0:T(1,128)S(1)} all-to-all(f32[8,1,2048]{2,1,0:T(1,128)S(1)} %bitcast.41), channel_id=1, replica_groups=mesh['frame'=16,'dom'=8,'coef'=4] {'dom'}, dimensions={0} | all-to-all | bytes 131072 | tf_op jit(solution)/shard_map/all_to_all | solution.py:249
  21.5 23.1 %all_to_all.84 = f32[16,1,2048]{2,1,0:T(1,128)S(1)} all-to-all(f32[16,1,2048]{2,1,0:T(1,128)S(1)} %bitcast.28), channel_id=1, replica_groups=mesh['frame'=16,'dom'=8,'coef'=4] {'frame'}, dimensions={0} | all-to-all | bytes 262144 | tf_op jit(solution)/shard_map/all_to_all | solution.py:249
  44.6 11.0 %all_to_all.85 = f32[8,1,2048]{2,1,0:T(1,128)S(1)} all-to-all(f32[8,1,2048]{2,1,0:T(1,128)S(1)} %bitcast.36), channel_id=1, replica_groups=mesh['frame'=16,'dom'=8,'coef'=4] {'dom'}, dimensions={0} | all-to-all | bytes 131072 | tf_op jit(solution)/shard_map/all_to_all | solution.py:249
  55.6 1.0 fwd0.1
  56.7 8.5 %all_to_all.86 = f32[4,1,5120]{2,1,0:T(1,128)S(1)} all-to-all(f32[4,1,5120]{2,1,0:T(1,128)S(1)} %bitcast.40), channel_id=1, replica_groups=mesh['frame'=16,'dom'=8,'coef'=4] {'coef'}, dimensions={0} | all-to-all | bytes 163840 | tf_op jit(solution)/shard_map/all_to_all | solution.py:249
  65.2 2.0 %back1.1 = (f32[128,128]{1,0:T(8,128)S(1)}, f32[32,128]{1,0:T(8,128)S(1)}, f32[8,128]{1,0:T(8,128)S(1)}) custom-call(f32[8,4096]{1,0:T(8,128)S(1)} %get-tuple-element.24.geom, f32[8,4096]{1,0:T(8,128)S(1)} %get-tuple-element.31.place, f32[8,4096]{1,0:T(8,128)S(1)} %get-tuple-element.32.high, bf16[96,256]{1,0:T(8,128)(2,1)S(1)} %get-tuple-element.33.picks, ...), custom_call_target="tpu_custom_call" | custom-call | tf_op jit(solution)/shard_map/back1/pallas_call | solution.py:30
  67.3 9.4 %all_to_all.87 = f32[8,1,2048]{2,1,0:T(1,128)S(1)} all-to-all(f32[8,1,2048]{2,1,0:T(1,128)S(1)} %bitcast.42), channel_id=1, replica_groups=mesh['frame'=16,'dom'=8,'coef'=4] {'dom'}, dimensions={0} | all-to-all | bytes 131072 | tf_op jit(solution)/shard_map/all_to_all | solution.py:249
  76.7 15.2 %all_to_all.88 = f32[16,1,2048]{2,1,0:T(1,128)S(1)} all-to-all(f32[16,1,2048]{2,1,0:T(1,128)S(1)} %bitcast.30), channel_id=1, replica_groups=mesh['frame'=16,'dom'=8,'coef'=4] {'frame'}, dimensions={0} | all-to-all | bytes 262144 | tf_op jit(solution)/shard_map/all_to_all | solution.py:249
  91.9 11.0 %all_to_all.89 = f32[8,1,2048]{2,1,0:T(1,128)S(1)} all-to-all(f32[8,1,2048]{2,1,0:T(1,128)S(1)} %bitcast.38), channel_id=1, replica_groups=mesh['frame'=16,'dom'=8,'coef'=4] {'dom'}, dimensions={0} | all-to-all | bytes 131072 | tf_op jit(solution)/shard_map/all_to_all | solution.py:249
  103.0 1.0 fwd1.1
  103.9 6.9 %all_to_all.90 = f32[4,1,5120]{2,1,0:T(1,128)S(1)} all-to-all(f32[4,1,5120]{2,1,0:T(1,128)S(1)} %bitcast.39), channel_id=1, replica_groups=mesh['frame'=16,'dom'=8,'coef'=4] {'coef'}, dimensions={0} | all-to-all | bytes 163840 | tf_op jit(solution)/shard_map/all_to_all | solution.py:249
  110.9 0.1 norm.1
  111.0 22.2 %all_to_all.91 = f32[128,1,128]{2,1,0:T(1,128)S(1)} all-to-all(f32[128,1,128]{2,1,0:T(1,128)S(1)} %bitcast.43), channel_id=1, replica_groups=mesh['frame'=16,'dom'=8,'coef'=4] {'frame','dom'}, dimensions={0} | all-to-all | bytes 131072 | tf_op jit(solution)/shard_map/all_to_all | solution.py:249
  133.1 0.8 last.1
  (4 shorter events, 0.1 us)
Async XLA Ops:
  0.6 0.9 copy-start
  1.5 0.9 copy-start.1
  2.4 0.9 copy-start.2
  3.3 0.7 copy-start.3
  4.1 0.7 copy-start.4

commit v4 on v3

--- a/solution.py
+++ b/solution.py
@@ -266,6 +266,7 @@
 
     sources = [geometry, fraction, interval, pattern, target.reshape(32, 128)]
     copies = [shape(s.shape, s.dtype) for s in sources]
+    sources = [pltpu.with_memory_space_constraint(s, pltpu.HBM) for s in sources]
     local, geom, frac, knot, patt, target, place, high, types = call(
         first_back,
         "back0",

time: 135 us -> 131 us (0.970)
  local copies, waits for them, and re-layouts: 4.11 us -> 0 us
    unnamed x10 -> x0, local copies, waits for them, and re-layouts: 4.11 us -> none
where the time goes in v4:
time: 131 us; the launch traced here: 130 us
  blocking collectives  121 us (92%)
  Pallas kernels  8.26 us (6%)
    all_to_all x9, blocking collectives, exchange(): lax.all_to_all(value.reshape(count, rows * 128 // count), axis, 0, 0, til...  121 us
    pallas_call x10, Pallas kernels, call(): pl.pallas_call(kernel, out_shape=outs, in_specs=[space] * len(args), out_...  8.26 us

profile of v4, /device:TPU:1, one launch (start us, length us, event | category | flops | bytes accessed | tf_op | source)
XLA Modules:
  0.0 130.4 jit_solution(14655287157931699507)
XLA Ops:
  0.6 3.2 %back0.1 = (f32[128,128]{1,0:T(8,128)S(1)}, f32[8,4096]{1,0:T(8,128)S(1)}, f32[8,4096]{1,0:T(8,128)S(1)}, s32[8,4096]{1,0:T(8,128)S(1)}, s32[8,32]{1,0:T(8,128)S...) custom-call(f32[8,4096]{1,0:T(8,128)} %refs_0_.1, ...), custom_call_target="tpu_custom_call" | custom-call | tf_op jit(solution)/shard_map/back0/pallas_call | solution.py:30
  3.9 14.1 %all_to_all.83 = f32[8,1,2048]{2,1,0:T(1,128)S(1)} all-to-all(f32[8,1,2048]{2,1,0:T(1,128)S(1)} %bitcast.41), channel_id=1, replica_groups=mesh['frame'=16,'dom'=8,'coef'=4] {'dom'}, dimensions={0} | all-to-all | bytes 131072 | tf_op jit(solution)/shard_map/all_to_all | solution.py:249
  18.0 23.1 %all_to_all.84 = f32[16,1,2048]{2,1,0:T(1,128)S(1)} all-to-all(f32[16,1,2048]{2,1,0:T(1,128)S(1)} %bitcast.28), channel_id=1, replica_groups=mesh['frame'=16,'dom'=8,'coef'=4] {'frame'}, dimensions={0} | all-to-all | bytes 262144 | tf_op jit(solution)/shard_map/all_to_all | solution.py:249
  41.0 11.0 %all_to_all.85 = f32[8,1,2048]{2,1,0:T(1,128)S(1)} all-to-all(f32[8,1,2048]{2,1,0:T(1,128)S(1)} %bitcast.36), channel_id=1, replica_groups=mesh['frame'=16,'dom'=8,'coef'=4] {'dom'}, dimensions={0} | all-to-all | bytes 131072 | tf_op jit(solution)/shard_map/all_to_all | solution.py:249
  52.1 1.0 fwd0.1
  53.1 8.5 %all_to_all.86 = f32[4,1,5120]{2,1,0:T(1,128)S(1)} all-to-all(f32[4,1,5120]{2,1,0:T(1,128)S(1)} %bitcast.40), channel_id=1, replica_groups=mesh['frame'=16,'dom'=8,'coef'=4] {'coef'}, dimensions={0} | all-to-all | bytes 163840 | tf_op jit(solution)/shard_map/all_to_all | solution.py:249
  61.6 2.0 %back1.1 = (f32[128,128]{1,0:T(8,128)S(1)}, f32[32,128]{1,0:T(8,128)S(1)}, f32[8,128]{1,0:T(8,128)S(1)}) custom-call(f32[8,4096]{1,0:T(8,128)S(1)} %get-tuple-element.24.geom, f32[8,4096]{1,0:T(8,128)S(1)} %get-tuple-element.31.place, f32[8,4096]{1,0:T(8,128)S(1)} %get-tuple-element.32.high, bf16[96,256]{1,0:T(8,128)(2,1)S(1)} %get-tuple-element.33.picks, ...), custom_call_target="tpu_custom_call" | custom-call | tf_op jit(solution)/shard_map/back1/pallas_call | solution.py:30
  63.7 9.4 %all_to_all.87 = f32[8,1,2048]{2,1,0:T(1,128)S(1)} all-to-all(f32[8,1,2048]{2,1,0:T(1,128)S(1)} %bitcast.42), channel_id=1, replica_groups=mesh['frame'=16,'dom'=8,'coef'=4] {'dom'}, dimensions={0} | all-to-all | bytes 131072 | tf_op jit(solution)/shard_map/all_to_all | solution.py:249
  73.1 15.2 %all_to_all.88 = f32[16,1,2048]{2,1,0:T(1,128)S(1)} all-to-all(f32[16,1,2048]{2,1,0:T(1,128)S(1)} %bitcast.30), channel_id=1, replica_groups=mesh['frame'=16,'dom'=8,'coef'=4] {'frame'}, dimensions={0} | all-to-all | bytes 262144 | tf_op jit(solution)/shard_map/all_to_all | solution.py:249
  88.3 11.0 %all_to_all.89 = f32[8,1,2048]{2,1,0:T(1,128)S(1)} all-to-all(f32[8,1,2048]{2,1,0:T(1,128)S(1)} %bitcast.38), channel_id=1, replica_groups=mesh['frame'=16,'dom'=8,'coef'=4] {'dom'}, dimensions={0} | all-to-all | bytes 131072 | tf_op jit(solution)/shard_map/all_to_all | solution.py:249
  99.4 1.0 fwd1.1
  100.3 6.9 %all_to_all.90 = f32[4,1,5120]{2,1,0:T(1,128)S(1)} all-to-all(f32[4,1,5120]{2,1,0:T(1,128)S(1)} %bitcast.39), channel_id=1, replica_groups=mesh['frame'=16,'dom'=8,'coef'=4] {'coef'}, dimensions={0} | all-to-all | bytes 163840 | tf_op jit(solution)/shard_map/all_to_all | solution.py:249
  107.3 0.1 norm.1
  107.4 22.2 %all_to_all.91 = f32[128,1,128]{2,1,0:T(1,128)S(1)} all-to-all(f32[128,1,128]{2,1,0:T(1,128)S(1)} %bitcast.43), channel_id=1, replica_groups=mesh['frame'=16,'dom'=8,'coef'=4] {'frame','dom'}, dimensions={0} | all-to-all | bytes 131072 | tf_op jit(solution)/shard_map/all_to_all | solution.py:249
  129.5 0.8 last.1
  (4 shorter events, 0.1 us)

commit v5 on v4

--- a/solution.py
+++ b/solution.py
@@ -200,11 +200,14 @@
     transposed(geom, place, high, picks, image, total, out, parts)
 
 
-def scattered(count, copies, got, out):
+def scattered(count, groups, copies, got, out):
     rows = got.shape[0] // count
-    total = parts_sum(got, count, rows)
-    for at in range(copies):
-        out[at * rows : (at + 1) * rows, :] = total
+    for group in range(groups):
+        total = got[group * rows : (group + 1) * rows, :]
+        for at in range(group + groups, count, groups):
+            total = total + got[at * rows : (at + 1) * rows, :]
+        for at in range(copies):
+            out[(at * groups + group) * rows : (at * groups + group + 1) * rows, :] = total
 
 
 def first_forward(geom, frac, knot, patt, grad, out, picks, shift, chosen):
@@ -251,17 +254,18 @@
 
 
 def on_device(geometry, fraction, interval, pattern, target):
-    frames, doms, coefs = lax.axis_size("frame"), lax.axis_size("dom"), lax.axis_size("coef")
-    piece = TABLE // doms
+    near = lax.axis_size("near")
+    frames, doms, coefs = lax.axis_size("far") * near, lax.axis_size("dom"), lax.axis_size("coef")
     shape = jax.ShapeDtypeStruct
     parts = pltpu.VMEM((8 * PAIRS, 128), F32)
     chosen = pltpu.VMEM((2 * PAIRS, 128), F32)
 
     def reduced(local):
-        got = exchange(local, "dom", doms)
-        (mine,) = call(functools.partial(scattered, doms, frames), "scatter_dom", [(frames * piece, 128)], [got])
-        got = exchange(mine, "frame", frames)
-        (mine,) = call(functools.partial(scattered, frames, doms), "scatter_frame", [(TABLE, 128)], [got])
+        got = exchange(local, ("dom", "near"), doms * near)
+        mine = frames * TABLE // (doms * near)
+        (mine,) = call(functools.partial(scattered, doms * near, 1, frames), "scatter_dom", [(mine, 128)], [got])
+        got = exchange(mine, ("far", "near"), frames)
+        (mine,) = call(functools.partial(scattered, frames, near, doms), "scatter_frame", [(TABLE, 128)], [got])
         return exchange(mine, "dom", doms)
 
     sources = [geometry, fraction, interval, pattern, target.reshape(32, 128)]
@@ -299,7 +303,7 @@
     local, image1, gamma1 = call(
         norm_kernel, "norm", [(frames * doms, 128), (32, 128), (8, 128)], [got, gamma0, image0]
     )
-    got = exchange(local, ("frame", "dom"), frames * doms)
+    got = exchange(local, ("far", "near", "dom"), frames * doms)
     sol, resid = call(
         last_kernel,
         "last",
@@ -310,12 +314,10 @@
 
 
 def solution(mesh):
-    in_specs = (
-        P("coef", ("frame", "dom")),
-        P("coef", ("frame", "dom")),
-        P("coef", ("frame", "dom")),
-        P("coef", ("frame", "dom")),
-        P(("frame", "dom")),
-    )
-    out_specs = (P("coef", None), P(("frame", "dom")))
+    frames, doms, coefs = mesh.devices.shape
+    near = 2 if frames % 2 == 0 else 1
+    mesh = jax.sharding.Mesh(mesh.devices.reshape(frames // near, near, doms, coefs), ("far", "near", "dom", "coef"))
+    rows = ("far", "near", "dom")
+    in_specs = (P("coef", rows), P("coef", rows), P("coef", rows), P("coef", rows), P(rows))
+    out_specs = (P("coef", None), P(rows))
     return jax.shard_map(on_device, mesh=mesh, in_specs=in_specs, out_specs=out_specs, check_vma=False)

time: 131 us -> 129 us (0.985)
  blocking collectives: 121 us -> 119 us
    all_to_all x9, blocking collectives: 121 us -> 119 us  [exchange(): lax.all_to_all(value.reshape(count, rows * 128 // count), axis, 0, 0, til...]
where the time goes in v5:
time: 129 us; the launch traced here: 128 us
  blocking collectives  119 us (92%)
  Pallas kernels  8.26 us (6%)
    all_to_all x9, blocking collectives, exchange(): lax.all_to_all(value.reshape(count, rows * 128 // count), axis, 0, 0, til...  119 us
    pallas_call x10, Pallas kernels, call(): pl.pallas_call(kernel, out_shape=outs, in_specs=[space] * len(args), out_...  8.26 us

profile of v5, /device:TPU:1, one launch (start us, length us, event | category | flops | bytes accessed | tf_op | source)
XLA Modules:
  0.0 128.3 jit_solution(4055948081837643746)
XLA Ops:
  0.6 3.2 %back0.1 = (f32[128,128]{1,0:T(8,128)S(1)}, f32[8,4096]{1,0:T(8,128)S(1)}, f32[8,4096]{1,0:T(8,128)S(1)}, s32[8,4096]{1,0:T(8,128)S(1)}, s32[8,32]{1,0:T(8,128)S...) custom-call(f32[8,4096]{1,0:T(8,128)} %refs_0_.1, ...), custom_call_target="tpu_custom_call" | custom-call | tf_op jit(solution)/shard_map/back0/pallas_call | solution.py:30
  3.9 15.2 %all_to_all.83 = f32[16,1,1024]{2,1,0:T(1,128)S(1)} all-to-all(f32[16,1,1024]{2,1,0:T(1,128)S(1)} %bitcast.41), channel_id=1, replica_groups=mesh['far'=8,'near'=2,'dom'=8,'coef'=4] {'dom','near'}, dimensions={0} | all-to-all | bytes 131072 | tf_op jit(solution)/shard_map/all_to_all | solution.py:252
  19.1 23.1 %all_to_all.84 = f32[16,1,1024]{2,1,0:T(1,128)S(1)} all-to-all(f32[16,1,1024]{2,1,0:T(1,128)S(1)} %bitcast.32), channel_id=1, replica_groups=mesh['far'=8,'near'=2,'dom'=8,'coef'=4] {'far','near'}, dimensions={0} | all-to-all | bytes 131072 | tf_op jit(solution)/shard_map/all_to_all | solution.py:252
  42.2 9.4 %all_to_all.85 = f32[8,1,2048]{2,1,0:T(1,128)S(1)} all-to-all(f32[8,1,2048]{2,1,0:T(1,128)S(1)} %bitcast.34), channel_id=1, replica_groups=mesh['far'=8,'near'=2,'dom'=8,'coef'=4] {'dom'}, dimensions={0} | all-to-all | bytes 131072 | tf_op jit(solution)/shard_map/all_to_all | solution.py:252
  51.6 1.0 fwd0.1
  52.6 8.5 %all_to_all.86 = f32[4,1,5120]{2,1,0:T(1,128)S(1)} all-to-all(f32[4,1,5120]{2,1,0:T(1,128)S(1)} %bitcast.40), channel_id=1, replica_groups=mesh['far'=8,'near'=2,'dom'=8,'coef'=4] {'coef'}, dimensions={0} | all-to-all | bytes 163840 | tf_op jit(solution)/shard_map/all_to_all | solution.py:252
  61.2 2.0 %back1.1 = (f32[128,128]{1,0:T(8,128)S(1)}, f32[32,128]{1,0:T(8,128)S(1)}, f32[8,128]{1,0:T(8,128)S(1)}) custom-call(f32[8,4096]{1,0:T(8,128)S(1)} %get-tuple-element.24.geom, f32[8,4096]{1,0:T(8,128)S(1)} %get-tuple-element.31.place, f32[8,4096]{1,0:T(8,128)S(1)} %get-tuple-element.32.high, bf16[96,256]{1,0:T(8,128)(2,1)S(1)} %get-tuple-element.33.picks, ...), custom_call_target="tpu_custom_call" | custom-call | tf_op jit(solution)/shard_map/back1/pallas_call | solution.py:30
  63.2 10.8 %all_to_all.87 = f32[16,1,1024]{2,1,0:T(1,128)S(1)} all-to-all(f32[16,1,1024]{2,1,0:T(1,128)S(1)} %bitcast.42), channel_id=1, replica_groups=mesh['far'=8,'near'=2,'dom'=8,'coef'=4] {'dom','near'}, dimensions={0} | all-to-all | bytes 131072 | tf_op jit(solution)/shard_map/all_to_all | solution.py:252
  74.0 14.5 %all_to_all.88 = f32[16,1,1024]{2,1,0:T(1,128)S(1)} all-to-all(f32[16,1,1024]{2,1,0:T(1,128)S(1)} %bitcast.36), channel_id=1, replica_groups=mesh['far'=8,'near'=2,'dom'=8,'coef'=4] {'far','near'}, dimensions={0} | all-to-all | bytes 131072 | tf_op jit(solution)/shard_map/all_to_all | solution.py:252
  88.6 9.4 %all_to_all.89 = f32[8,1,2048]{2,1,0:T(1,128)S(1)} all-to-all(f32[8,1,2048]{2,1,0:T(1,128)S(1)} %bitcast.38), channel_id=1, replica_groups=mesh['far'=8,'near'=2,'dom'=8,'coef'=4] {'dom'}, dimensions={0} | all-to-all | bytes 131072 | tf_op jit(solution)/shard_map/all_to_all | solution.py:252
  98.0 1.0 fwd1.1
  98.9 6.9 %all_to_all.90 = f32[4,1,5120]{2,1,0:T(1,128)S(1)} all-to-all(f32[4,1,5120]{2,1,0:T(1,128)S(1)} %bitcast.39), channel_id=1, replica_groups=mesh['far'=8,'near'=2,'dom'=8,'coef'=4] {'coef'}, dimensions={0} | all-to-all | bytes 163840 | tf_op jit(solution)/shard_map/all_to_all | solution.py:252
  105.8 0.1 norm.1
  105.9 21.6 %all_to_all.91 = f32[128,1,128]{2,1,0:T(1,128)S(1)} all-to-all(f32[128,1,128]{2,1,0:T(1,128)S(1)} %bitcast.43), channel_id=1, replica_groups=mesh['far'=8,'near'=2,'dom'=8,'coef'=4] {'far','near','dom'}, dimensions={0} | all-to-all | bytes 131072 | tf_op jit(solution)/shard_map/all_to_all | solution.py:252
  127.5 0.8 last.1
  (4 shorter events, 0.1 us)

commit v6 on v5

--- a/solution.py
+++ b/solution.py
@@ -15,7 +15,8 @@
 TABLE = 128
 PAIRS = 256
 IMAGE = 40
-UNROLL = 8
+UNROLL = 16
+GROUP = 8
 TILES_DEV = 32
 
 VMEM = pl.BlockSpec(memory_space=pltpu.VMEM)
@@ -76,7 +77,14 @@
     picks_ref[...] = jnp.transpose(jnp.concatenate(picks, axis=0))[0:TD, :].astype(BF16)
 
 
-def transposed(geom_ref, place_ref, high_ref, picks_ref, resid_ref, total, out_ref, parts_ref):
+def spreading(spread_ref):
+    source = lax.broadcasted_iota(I32, (256, 256), 0)
+    column = lax.broadcasted_iota(I32, (256, 256), 1)
+    knot = jnp.where(column >= 128, 128 + (column & 31), column)
+    spread_ref[...] = jnp.where(5 * (source & 31) + (source >> 5) == knot, 1.0, 0.0).astype(BF16)
+
+
+def transposed(geom_ref, place_ref, high_ref, picks_ref, spread_ref, shape_ref, resid_ref, total, out_ref, parts_ref):
     places = lax.broadcasted_iota(I32, (8, 128), 0).astype(F32)
     rows = lax.broadcasted_iota(I32, (2, 16, 128), 0) * 16 + lax.broadcasted_iota(I32, (2, 16, 128), 1)
     rows = rows.astype(F32).astype(BF16)
@@ -90,11 +98,16 @@
             values, hits = [], []
             for half in range(2):
                 s = slice(2 * pair + half, 2 * pair + half + 1)
-                near = jnp.abs(jnp.broadcast_to(place_ref[s, lanes], (8, 128)) - places)
-                a = jnp.maximum(2.0 - near, 0.0)
-                b = jnp.maximum(1.0 - near, 0.0)
-                amount = jnp.broadcast_to(geom_ref[s, lanes], (8, 128)) * resid
-                value = amount * (a * a * a - (4.0 * b) * (b * b))
+                kept = pl.ds(pl.multiple_of((t * 8 + 2 * pair + half) * 8, 8), 8)
+                if place_ref is None:
+                    spline = shape_ref[kept, :]
+                else:
+                    near = jnp.abs(jnp.broadcast_to(place_ref[s, lanes], (8, 128)) - places)
+                    a = jnp.maximum(2.0 - near, 0.0)
+                    b = jnp.maximum(1.0 - near, 0.0)
+                    spline = a * a * a - (4.0 * b) * (b * b)
+                    shape_ref[kept, :] = spline
+                value = jnp.broadcast_to(geom_ref[s, lanes], (8, 128)) * resid * spline
                 rounded = value.astype(BF16).astype(F32)
                 values.append(jnp.concatenate([rounded, value - rounded], axis=0).astype(BF16))
                 at = jnp.broadcast_to(high_ref[s, lanes], (16, 128)).astype(BF16)
@@ -126,10 +139,7 @@
         halves.append(piece)
     high, low = split(jnp.concatenate(halves, axis=1))
     grad = jnp.dot(picks, high, preferred_element_type=F32) + jnp.dot(picks, low, preferred_element_type=F32)
-    source = lax.broadcasted_iota(I32, (256, 256), 0)
-    column = lax.broadcasted_iota(I32, (256, 256), 1)
-    knot = jnp.where(column >= 128, 128 + (column & 31), column)
-    spread = jnp.where(5 * (source & 31) + (source >> 5) == knot, 1.0, 0.0).astype(BF16)
+    spread = spread_ref[...]
     high, low = split(grad)
     grad = jnp.dot(high, spread, preferred_element_type=F32) + jnp.dot(low, spread, preferred_element_type=F32)
     out_ref[0:TD, :] = grad[:, 0:128]
@@ -150,21 +160,27 @@
         low_rows.append(jnp.where(lane == kind, 1.0, 0.0))
         high_rows.append(jnp.where(lane == TD + kind - HIGH * block, 1.0, 0.0))
         shift_ref[8 * t : 8 * t + 8, :] = 32 * block
-    picks_ref[...] = jnp.concatenate(low_rows + high_rows, axis=0).astype(BF16)
-
-
-def applied(geom_ref, frac_ref, knot_ref, picks_ref, shift_ref, table, out_ref, chosen_ref):
-    picks = picks_ref[...]
-    high, low = split(table)
-    chosen_ref[...] = jnp.dot(picks, high, preferred_element_type=F32) + jnp.dot(
-        picks, low, preferred_element_type=F32
-    )
+    rows = []
+    for t in range(0, TILES_DEV, GROUP):
+        rows += low_rows[t : t + GROUP] + high_rows[t : t + GROUP]
+    picks_ref[...] = jnp.concatenate(rows, axis=0).astype(BF16)
+
+
+def applied(geom_ref, frac_ref, knot_ref, picks_ref, shift_ref, table, out_ref):
+    both = jnp.concatenate(split(table), axis=1)
+    gamma = jnp.broadcast_to(total_of(table[0:KNOTS] * table[0:KNOTS]), (8, 128))
+    for c in range(out_ref.shape[0] // IMAGE):
+        out_ref[c * IMAGE + 32 : (c + 1) * IMAGE, :] = gamma
     for t in range(TILES_DEV):
+        if t % GROUP == 0:
+            got = jnp.dot(picks_ref[16 * t : 16 * (t + GROUP), :], both, preferred_element_type=F32)
+            chosen = got[:, 0:128] + got[:, 128:256]
         lanes = slice(128 * t, 128 * (t + 1))
         slots = slice(8 * t, 8 * t + 8)
+        at = 8 * (t % GROUP)
+        first = chosen[at : at + 8]
+        last = chosen[8 * GROUP + at : 8 * GROUP + at + 8]
         base = knot_ref[:, lanes]
-        first = chosen_ref[slots, :]
-        last = chosen_ref[PAIRS + 8 * t : PAIRS + 8 * t + 8, :]
         value = None
         for j, weight in enumerate(weights(frac_ref[:, lanes])):
             at = base + j
@@ -175,29 +191,28 @@
         row = jnp.sum(geom_ref[:, lanes] * value, axis=0, keepdims=True)
         for c in range(out_ref.shape[0] // IMAGE):
             out_ref[c * IMAGE + t : c * IMAGE + t + 1, :] = row
-    gamma = jnp.broadcast_to(total_of(table[0:KNOTS] * table[0:KNOTS]), (8, 128))
-    for c in range(out_ref.shape[0] // IMAGE):
-        out_ref[c * IMAGE + 32 : (c + 1) * IMAGE, :] = gamma
 
 
 def first_back(*refs):
-    sources, (out, *copies), (place, high, picks), (parts, sems) = refs[:5], refs[5:11], refs[11:14], refs[14:]
+    sources, (out, *copies), (high, picks, spread, splines) = refs[:5], refs[5:11], refs[11:15]
+    place, parts, sems = refs[15:]
     moves = [pltpu.make_async_copy(a, b, sems.at[i]) for i, (a, b) in enumerate(zip(sources, copies, strict=True))]
     for move in moves:
         move.start()
+    spreading(spread)
     for move in moves:
         move.wait()
     geom, frac, knot, patt, target = copies
     prepare(frac, knot, patt, place, high, picks)
-    transposed(geom, place, high, picks, target, 0.0, out, parts)
-
-
-def later_back(geom, place, high, picks, got, out, image, gamma, parts):
+    transposed(geom, place, high, picks, spread, splines, target, 0.0, out, parts)
+
+
+def later_back(geom, high, picks, spread, splines, got, out, image, gamma, parts):
     whole = parts_sum(got, got.shape[0] // IMAGE, IMAGE)
     image[...] = whole[0:32]
     gamma[...] = whole[32:40]
     total = jnp.broadcast_to(total_of(whole[0:32] * whole[0:32]), (8, 128))
-    transposed(geom, place, high, picks, image, total, out, parts)
+    transposed(geom, None, high, picks, spread, splines, image, total, out, parts)
 
 
 def scattered(count, groups, copies, got, out):
@@ -210,15 +225,15 @@
             out[(at * groups + group) * rows : (at * groups + group + 1) * rows, :] = total
 
 
-def first_forward(geom, frac, knot, patt, grad, out, picks, shift, chosen):
+def first_forward(geom, frac, knot, patt, grad, out, picks, shift):
     choose(patt, picks, shift)
-    applied(geom, frac, knot, picks, shift, grad[...], out, chosen)
-
-
-def later_forward(geom, frac, knot, picks, shift, grad, other, gamma, out, table, chosen):
+    applied(geom, frac, knot, picks, shift, grad[...], out)
+
+
+def later_forward(geom, frac, knot, picks, shift, grad, other, gamma, out, table):
     alpha = gamma[0:1, :] / other[KNOTS : KNOTS + 1, :]
     table[...] = grad[...] - alpha * other[...]
-    applied(geom, frac, knot, picks, shift, table[...], out, chosen)
+    applied(geom, frac, knot, picks, shift, table[...], out)
 
 
 def norm_kernel(got, gamma, image, out, image_out, gamma_out):
@@ -258,7 +273,6 @@
     frames, doms, coefs = lax.axis_size("far") * near, lax.axis_size("dom"), lax.axis_size("coef")
     shape = jax.ShapeDtypeStruct
     parts = pltpu.VMEM((8 * PAIRS, 128), F32)
-    chosen = pltpu.VMEM((2 * PAIRS, 128), F32)
 
     def reduced(local):
         got = exchange(local, ("dom", "near"), doms * near)
@@ -271,12 +285,12 @@
     sources = [geometry, fraction, interval, pattern, target.reshape(32, 128)]
     copies = [shape(s.shape, s.dtype) for s in sources]
     sources = [pltpu.with_memory_space_constraint(s, pltpu.HBM) for s in sources]
-    local, geom, frac, knot, patt, target, place, high, types = call(
+    local, geom, frac, knot, patt, target, high, types, spread, splines = call(
         first_back,
         "back0",
-        [(TABLE, 128), *copies, (8, 4096), (8, 4096), shape((TD, PAIRS), BF16)],
+        [(TABLE, 128), *copies, (8, 4096), shape((TD, PAIRS), BF16), shape((256, 256), BF16), (8 * PAIRS, 128)],
         sources,
-        [parts, pltpu.SemaphoreType.DMA((5,))],
+        [pltpu.VMEM((8, 4096), F32), parts, pltpu.SemaphoreType.DMA((5,))],
         HBM,
     )
     grad0 = reduced(local)
@@ -285,11 +299,10 @@
         "fwd0",
         [(coefs * IMAGE, 128), shape((2 * PAIRS, 128), BF16), shape((PAIRS, 128), I32)],
         [geom, frac, knot, patt, grad0],
-        [chosen],
     )
     got = exchange(local, "coef", coefs)
     local, image0, gamma0 = call(
-        later_back, "back1", [(TABLE, 128), (32, 128), (8, 128)], [geom, place, high, types, got], [parts]
+        later_back, "back1", [(TABLE, 128), (32, 128), (8, 128)], [geom, high, types, spread, splines, got], [parts]
     )
     other = reduced(local)
     local, grad1 = call(
@@ -297,7 +310,6 @@
         "fwd1",
         [(coefs * IMAGE, 128), (TABLE, 128)],
         [geom, frac, knot, picks, shift, grad0, other, gamma0],
-        [chosen],
     )
     got = exchange(local, "coef", coefs)
     local, image1, gamma1 = call(

time: 129 us -> 128 us (level)
  no operation moved by 1% of the time
where the time goes in v6:
time: 128 us
  blocking collectives  119 us (93%)
  Pallas kernels  7.53 us (6%)
    all_to_all x9, blocking collectives, exchange(): lax.all_to_all(value.reshape(count, rows * 128 // count), axis, 0, 0, til...  119 us
    pallas_call x10, Pallas kernels, call(): pl.pallas_call(kernel, out_shape=outs, in_specs=[space] * len(args), out_...  7.53 us

profile of v6, /device:TPU:1, one launch (start us, length us, event | category | flops | bytes accessed | tf_op | source)
XLA Modules:
  0.0 127.6 jit_solution(1098681727306720213)
XLA Ops:
  0.6 3.0 %back0.1 = (f32[128,128]{1,0:T(8,128)S(1)}, f32[8,4096]{1,0:T(8,128)S(1)}, f32[8,4096]{1,0:T(8,128)S(1)}, s32[8,4096]{1,0:T(8,128)S(1)}, s32[8,32]{1,0:T(8,128)S...) custom-call(f32[8,4096]{1,0:T(8,128)} %refs_0_.1, ...), custom_call_target="tpu_custom_call" | custom-call | tf_op jit(solution)/shard_map/back0/pallas_call | solution.py:31
  3.6 15.2 %all_to_all.83 = f32[16,1,1024]{2,1,0:T(1,128)S(1)} all-to-all(f32[16,1,1024]{2,1,0:T(1,128)S(1)} %bitcast.41), channel_id=1, replica_groups=mesh['far'=8,'near'=2,'dom'=8,'coef'=4] {'dom','near'}, dimensions={0} | all-to-all | bytes 131072 | tf_op jit(solution)/shard_map/all_to_all | solution.py:267
  18.9 23.1 %all_to_all.84 = f32[16,1,1024]{2,1,0:T(1,128)S(1)} all-to-all(f32[16,1,1024]{2,1,0:T(1,128)S(1)} %bitcast.32), channel_id=1, replica_groups=mesh['far'=8,'near'=2,'dom'=8,'coef'=4] {'far','near'}, dimensions={0} | all-to-all | bytes 131072 | tf_op jit(solution)/shard_map/all_to_all | solution.py:267
  42.0 9.4 %all_to_all.85 = f32[8,1,2048]{2,1,0:T(1,128)S(1)} all-to-all(f32[8,1,2048]{2,1,0:T(1,128)S(1)} %bitcast.34), channel_id=1, replica_groups=mesh['far'=8,'near'=2,'dom'=8,'coef'=4] {'dom'}, dimensions={0} | all-to-all | bytes 131072 | tf_op jit(solution)/shard_map/all_to_all | solution.py:267
  51.4 1.0 fwd0.1
  52.4 8.6 %all_to_all.86 = f32[4,1,5120]{2,1,0:T(1,128)S(1)} all-to-all(f32[4,1,5120]{2,1,0:T(1,128)S(1)} %bitcast.40), channel_id=1, replica_groups=mesh['far'=8,'near'=2,'dom'=8,'coef'=4] {'coef'}, dimensions={0} | all-to-all | bytes 163840 | tf_op jit(solution)/shard_map/all_to_all | solution.py:267
  61.0 1.5 %back1.1 = (f32[128,128]{1,0:T(8,128)S(1)}, f32[32,128]{1,0:T(8,128)S(1)}, f32[8,128]{1,0:T(8,128)S(1)}) custom-call(f32[8,4096]{1,0:T(8,128)S(1)} %get-tuple-element.25.geom, f32[8,4096]{1,0:T(8,128)S(1)} %get-tuple-element.32.high, bf16[96,256]{1,0:T(8,128)(2,1)S(1)} %get-tuple-element.33.picks, bf16[256,256]{1,0:T(8,128)(2,1)S(1)} %get-tuple-element.34.spread, ...), custom_call_target="tpu_custom_call" | custom-call | tf_op jit(solution)/shard_map/back1/pallas_call | solution.py:31
  62.5 10.8 %all_to_all.87 = f32[16,1,1024]{2,1,0:T(1,128)S(1)} all-to-all(f32[16,1,1024]{2,1,0:T(1,128)S(1)} %bitcast.42), channel_id=1, replica_groups=mesh['far'=8,'near'=2,'dom'=8,'coef'=4] {'dom','near'}, dimensions={0} | all-to-all | bytes 131072 | tf_op jit(solution)/shard_map/all_to_all | solution.py:267
  73.3 14.5 %all_to_all.88 = f32[16,1,1024]{2,1,0:T(1,128)S(1)} all-to-all(f32[16,1,1024]{2,1,0:T(1,128)S(1)} %bitcast.36), channel_id=1, replica_groups=mesh['far'=8,'near'=2,'dom'=8,'coef'=4] {'far','near'}, dimensions={0} | all-to-all | bytes 131072 | tf_op jit(solution)/shard_map/all_to_all | solution.py:267
  87.8 9.4 %all_to_all.89 = f32[8,1,2048]{2,1,0:T(1,128)S(1)} all-to-all(f32[8,1,2048]{2,1,0:T(1,128)S(1)} %bitcast.38), channel_id=1, replica_groups=mesh['far'=8,'near'=2,'dom'=8,'coef'=4] {'dom'}, dimensions={0} | all-to-all | bytes 131072 | tf_op jit(solution)/shard_map/all_to_all | solution.py:267
  97.2 1.0 fwd1.1
  98.2 6.9 %all_to_all.90 = f32[4,1,5120]{2,1,0:T(1,128)S(1)} all-to-all(f32[4,1,5120]{2,1,0:T(1,128)S(1)} %bitcast.39), channel_id=1, replica_groups=mesh['far'=8,'near'=2,'dom'=8,'coef'=4] {'coef'}, dimensions={0} | all-to-all | bytes 163840 | tf_op jit(solution)/shard_map/all_to_all | solution.py:267
  105.1 0.1 norm.1
  105.2 21.6 %all_to_all.91 = f32[128,1,128]{2,1,0:T(1,128)S(1)} all-to-all(f32[128,1,128]{2,1,0:T(1,128)S(1)} %bitcast.43), channel_id=1, replica_groups=mesh['far'=8,'near'=2,'dom'=8,'coef'=4] {'far','near','dom'}, dimensions={0} | all-to-all | bytes 131072 | tf_op jit(solution)/shard_map/all_to_all | solution.py:267
  126.8 0.8 last.1
  (4 shorter events, 0.1 us)

commit v7 on v6

--- a/solution.py
+++ b/solution.py
@@ -151,42 +151,34 @@
     out_ref[KNOTS:TABLE, :] = jnp.where(sub == 0, total, 0.0)
 
 
-def choose(patt_ref, picks_ref, shift_ref):
+def choose(patt_ref, picks_ref):
     lane = lax.broadcasted_iota(I32, (8, 128), 1)
-    low_rows, high_rows = [], []
-    for t in range(TILES_DEV):
-        kind = jnp.broadcast_to(patt_ref[:, t : t + 1], (8, 128))
-        block = jnp.where(kind >= HIGH, 1, 0) + jnp.where(kind >= 2 * HIGH, 1, 0) + jnp.where(kind >= 3 * HIGH, 1, 0)
-        low_rows.append(jnp.where(lane == kind, 1.0, 0.0))
-        high_rows.append(jnp.where(lane == TD + kind - HIGH * block, 1.0, 0.0))
-        shift_ref[8 * t : 8 * t + 8, :] = 32 * block
-    rows = []
-    for t in range(0, TILES_DEV, GROUP):
-        rows += low_rows[t : t + GROUP] + high_rows[t : t + GROUP]
+    rows = [jnp.where(lane == patt_ref[:, t : t + 1], 1.0, 0.0) for t in range(TILES_DEV)]
     picks_ref[...] = jnp.concatenate(rows, axis=0).astype(BF16)
 
 
-def applied(geom_ref, frac_ref, knot_ref, picks_ref, shift_ref, table, out_ref):
-    both = jnp.concatenate(split(table), axis=1)
+def applied(geom_ref, frac_ref, knot_ref, picks_ref, table, out_ref):
+    packed = table[TD:KNOTS]
+    tops = [packed] + [pltpu.roll(packed, 128 - 32 * q, 1) for q in range(1, 4)]
+    tops = jnp.concatenate(tops + [jnp.zeros((TABLE - TD, 128), F32)], axis=0)
+    both = jnp.concatenate([*split(table), *split(tops)], axis=1)
     gamma = jnp.broadcast_to(total_of(table[0:KNOTS] * table[0:KNOTS]), (8, 128))
     for c in range(out_ref.shape[0] // IMAGE):
         out_ref[c * IMAGE + 32 : (c + 1) * IMAGE, :] = gamma
     for t in range(TILES_DEV):
         if t % GROUP == 0:
-            got = jnp.dot(picks_ref[16 * t : 16 * (t + GROUP), :], both, preferred_element_type=F32)
-            chosen = got[:, 0:128] + got[:, 128:256]
+            got = jnp.dot(picks_ref[8 * t : 8 * (t + GROUP), :], both, preferred_element_type=F32)
+            bottoms = got[:, 0:128] + got[:, 128:256]
+            uppers = got[:, 256:384] + got[:, 384:512]
         lanes = slice(128 * t, 128 * (t + 1))
-        slots = slice(8 * t, 8 * t + 8)
-        at = 8 * (t % GROUP)
-        first = chosen[at : at + 8]
-        last = chosen[8 * GROUP + at : 8 * GROUP + at + 8]
+        slots = slice(8 * (t % GROUP), 8 * (t % GROUP) + 8)
         base = knot_ref[:, lanes]
         value = None
         for j, weight in enumerate(weights(frac_ref[:, lanes])):
-            at = base + j
-            near = jnp.take_along_axis(first, at & 127, axis=1, mode="promise_in_bounds")
-            far = jnp.take_along_axis(last, (at & 31) + shift_ref[slots, :], axis=1, mode="promise_in_bounds")
-            term = weight * jnp.where(at >= 128, far, near)
+            at = (base + j) & 127
+            near = jnp.take_along_axis(bottoms[slots], at, axis=1, mode="promise_in_bounds")
+            far = jnp.take_along_axis(uppers[slots], at, axis=1, mode="promise_in_bounds")
+            term = weight * jnp.where(base >= 128 - j, far, near)
             value = term if j == 0 else value + term
         row = jnp.sum(geom_ref[:, lanes] * value, axis=0, keepdims=True)
         for c in range(out_ref.shape[0] // IMAGE):
@@ -225,15 +217,15 @@
             out[(at * groups + group) * rows : (at * groups + group + 1) * rows, :] = total
 
 
-def first_forward(geom, frac, knot, patt, grad, out, picks, shift):
-    choose(patt, picks, shift)
-    applied(geom, frac, knot, picks, shift, grad[...], out)
-
-
-def later_forward(geom, frac, knot, picks, shift, grad, other, gamma, out, table):
+def first_forward(geom, frac, knot, patt, grad, out, picks):
+    choose(patt, picks)
+    applied(geom, frac, knot, picks, grad[...], out)
+
+
+def later_forward(geom, frac, knot, picks, grad, other, gamma, out, table):
     alpha = gamma[0:1, :] / other[KNOTS : KNOTS + 1, :]
     table[...] = grad[...] - alpha * other[...]
-    applied(geom, frac, knot, picks, shift, table[...], out)
+    applied(geom, frac, knot, picks, table[...], out)
 
 
 def norm_kernel(got, gamma, image, out, image_out, gamma_out):
@@ -294,10 +286,10 @@
         HBM,
     )
     grad0 = reduced(local)
-    local, picks, shift = call(
+    local, picks = call(
         first_forward,
         "fwd0",
-        [(coefs * IMAGE, 128), shape((2 * PAIRS, 128), BF16), shape((PAIRS, 128), I32)],
+        [(coefs * IMAGE, 128), shape((PAIRS, 128), BF16)],
         [geom, frac, knot, patt, grad0],
     )
     got = exchange(local, "coef", coefs)
@@ -309,7 +301,7 @@
         later_forward,
         "fwd1",
         [(coefs * IMAGE, 128), (TABLE, 128)],
-        [geom, frac, knot, picks, shift, grad0, other, gamma0],
+        [geom, frac, knot, picks, grad0, other, gamma0],
     )
     got = exchange(local, "coef", coefs)
     local, image1, gamma1 = call(

time: 128 us -> 128 us (level)
  no operation moved by 1% of the time
where the time goes in v7:
time: 128 us; the launch traced here: 127 us
  blocking collectives  119 us (93%)
  Pallas kernels  7.37 us (6%)
    all_to_all x9, blocking collectives, exchange(): lax.all_to_all(value.reshape(count, rows * 128 // count), axis, 0, 0, til...  119 us
    pallas_call x10, Pallas kernels, call(): pl.pallas_call(kernel, out_shape=outs, in_specs=[space] * len(args), out_...  7.37 us

profile of v7, /device:TPU:1, one launch (start us, length us, event | category | flops | bytes accessed | tf_op | source)
XLA Modules:
  0.0 127.5 jit_solution(10997135286359239334)
XLA Ops:
  0.6 3.0 %back0.1 = (f32[128,128]{1,0:T(8,128)S(1)}, f32[8,4096]{1,0:T(8,128)S(1)}, f32[8,4096]{1,0:T(8,128)S(1)}, s32[8,4096]{1,0:T(8,128)S(1)}, s32[8,32]{1,0:T(8,128)S...) custom-call(f32[8,4096]{1,0:T(8,128)} %refs_0_.1, ...), custom_call_target="tpu_custom_call" | custom-call | tf_op jit(solution)/shard_map/back0/pallas_call | solution.py:31
  3.6 15.2 %all_to_all.83 = f32[16,1,1024]{2,1,0:T(1,128)S(1)} all-to-all(f32[16,1,1024]{2,1,0:T(1,128)S(1)} %bitcast.41), channel_id=1, replica_groups=mesh['far'=8,'near'=2,'dom'=8,'coef'=4] {'dom','near'}, dimensions={0} | all-to-all | bytes 131072 | tf_op jit(solution)/shard_map/all_to_all | solution.py:259
  18.9 23.1 %all_to_all.84 = f32[16,1,1024]{2,1,0:T(1,128)S(1)} all-to-all(f32[16,1,1024]{2,1,0:T(1,128)S(1)} %bitcast.32), channel_id=1, replica_groups=mesh['far'=8,'near'=2,'dom'=8,'coef'=4] {'far','near'}, dimensions={0} | all-to-all | bytes 131072 | tf_op jit(solution)/shard_map/all_to_all | solution.py:259
  42.0 9.4 %all_to_all.85 = f32[8,1,2048]{2,1,0:T(1,128)S(1)} all-to-all(f32[8,1,2048]{2,1,0:T(1,128)S(1)} %bitcast.34), channel_id=1, replica_groups=mesh['far'=8,'near'=2,'dom'=8,'coef'=4] {'dom'}, dimensions={0} | all-to-all | bytes 131072 | tf_op jit(solution)/shard_map/all_to_all | solution.py:259
  51.4 0.9 fwd0.1
  52.3 8.6 %all_to_all.86 = f32[4,1,5120]{2,1,0:T(1,128)S(1)} all-to-all(f32[4,1,5120]{2,1,0:T(1,128)S(1)} %bitcast.40), channel_id=1, replica_groups=mesh['far'=8,'near'=2,'dom'=8,'coef'=4] {'coef'}, dimensions={0} | all-to-all | bytes 163840 | tf_op jit(solution)/shard_map/all_to_all | solution.py:259
  60.9 1.5 %back1.1 = (f32[128,128]{1,0:T(8,128)S(1)}, f32[32,128]{1,0:T(8,128)S(1)}, f32[8,128]{1,0:T(8,128)S(1)}) custom-call(f32[8,4096]{1,0:T(8,128)S(1)} %get-tuple-element.24.geom, f32[8,4096]{1,0:T(8,128)S(1)} %get-tuple-element.30.high, bf16[96,256]{1,0:T(8,128)(2,1)S(1)} %get-tuple-element.31.picks, bf16[256,256]{1,0:T(8,128)(2,1)S(1)} %get-tuple-element.32.spread, ...), custom_call_target="tpu_custom_call" | custom-call | tf_op jit(solution)/shard_map/back1/pallas_call | solution.py:31
  62.4 10.8 %all_to_all.87 = f32[16,1,1024]{2,1,0:T(1,128)S(1)} all-to-all(f32[16,1,1024]{2,1,0:T(1,128)S(1)} %bitcast.42), channel_id=1, replica_groups=mesh['far'=8,'near'=2,'dom'=8,'coef'=4] {'dom','near'}, dimensions={0} | all-to-all | bytes 131072 | tf_op jit(solution)/shard_map/all_to_all | solution.py:259
  73.2 14.5 %all_to_all.88 = f32[16,1,1024]{2,1,0:T(1,128)S(1)} all-to-all(f32[16,1,1024]{2,1,0:T(1,128)S(1)} %bitcast.36), channel_id=1, replica_groups=mesh['far'=8,'near'=2,'dom'=8,'coef'=4] {'far','near'}, dimensions={0} | all-to-all | bytes 131072 | tf_op jit(solution)/shard_map/all_to_all | solution.py:259
  87.8 9.4 %all_to_all.89 = f32[8,1,2048]{2,1,0:T(1,128)S(1)} all-to-all(f32[8,1,2048]{2,1,0:T(1,128)S(1)} %bitcast.38), channel_id=1, replica_groups=mesh['far'=8,'near'=2,'dom'=8,'coef'=4] {'dom'}, dimensions={0} | all-to-all | bytes 131072 | tf_op jit(solution)/shard_map/all_to_all | solution.py:259
  97.1 0.9 fwd1.1
  98.0 6.9 %all_to_all.90 = f32[4,1,5120]{2,1,0:T(1,128)S(1)} all-to-all(f32[4,1,5120]{2,1,0:T(1,128)S(1)} %bitcast.39), channel_id=1, replica_groups=mesh['far'=8,'near'=2,'dom'=8,'coef'=4] {'coef'}, dimensions={0} | all-to-all | bytes 163840 | tf_op jit(solution)/shard_map/all_to_all | solution.py:259
  105.0 0.1 norm.1
  105.1 21.6 %all_to_all.91 = f32[128,1,128]{2,1,0:T(1,128)S(1)} all-to-all(f32[128,1,128]{2,1,0:T(1,128)S(1)} %bitcast.43), channel_id=1, replica_groups=mesh['far'=8,'near'=2,'dom'=8,'coef'=4] {'far','near','dom'}, dimensions={0} | all-to-all | bytes 131072 | tf_op jit(solution)/shard_map/all_to_all | solution.py:259
  126.6 0.8 last.1
  (4 shorter events, 0.1 us)

commit v8 on v7

--- a/solution.py
+++ b/solution.py
@@ -189,13 +189,15 @@
     sources, (out, *copies), (high, picks, spread, splines) = refs[:5], refs[5:11], refs[11:15]
     place, parts, sems = refs[15:]
     moves = [pltpu.make_async_copy(a, b, sems.at[i]) for i, (a, b) in enumerate(zip(sources, copies, strict=True))]
-    for move in moves:
-        move.start()
+    for at in (1, 2, 3, 0, 4):
+        moves[at].start()
     spreading(spread)
-    for move in moves:
-        move.wait()
     geom, frac, knot, patt, target = copies
+    for at in (1, 2, 3):
+        moves[at].wait()
     prepare(frac, knot, patt, place, high, picks)
+    for at in (0, 4):
+        moves[at].wait()
     transposed(geom, place, high, picks, spread, splines, target, 0.0, out, parts)
 
 

time: 128 us -> 128 us (level)
  no operation moved by 1% of the time
where the time goes in v8:
time: 128 us; the launch traced here: 127 us
  blocking collectives  119 us (93%)
  Pallas kernels  7.31 us (6%)
    all_to_all x9, blocking collectives, exchange(): lax.all_to_all(value.reshape(count, rows * 128 // count), axis, 0, 0, til...  119 us
    pallas_call x10, Pallas kernels, call(): pl.pallas_call(kernel, out_shape=outs, in_specs=[space] * len(args), out_...  7.31 us

profile of v8, /device:TPU:1, one launch (start us, length us, event | category | flops | bytes accessed | tf_op | source)
XLA Modules:
  0.0 127.4 jit_solution(3625327931713851154)
XLA Ops:
  0.6 2.9 %back0.1 = (f32[128,128]{1,0:T(8,128)S(1)}, f32[8,4096]{1,0:T(8,128)S(1)}, f32[8,4096]{1,0:T(8,128)S(1)}, s32[8,4096]{1,0:T(8,128)S(1)}, s32[8,32]{1,0:T(8,128)S...) custom-call(f32[8,4096]{1,0:T(8,128)} %refs_0_.1, ...), custom_call_target="tpu_custom_call" | custom-call | tf_op jit(solution)/shard_map/back0/pallas_call | solution.py:31
  3.6 15.2 %all_to_all.83 = f32[16,1,1024]{2,1,0:T(1,128)S(1)} all-to-all(f32[16,1,1024]{2,1,0:T(1,128)S(1)} %bitcast.41), channel_id=1, replica_groups=mesh['far'=8,'near'=2,'dom'=8,'coef'=4] {'dom','near'}, dimensions={0} | all-to-all | bytes 131072 | tf_op jit(solution)/shard_map/all_to_all | solution.py:261
  18.9 23.1 %all_to_all.84 = f32[16,1,1024]{2,1,0:T(1,128)S(1)} all-to-all(f32[16,1,1024]{2,1,0:T(1,128)S(1)} %bitcast.32), channel_id=1, replica_groups=mesh['far'=8,'near'=2,'dom'=8,'coef'=4] {'far','near'}, dimensions={0} | all-to-all | bytes 131072 | tf_op jit(solution)/shard_map/all_to_all | solution.py:261
  41.9 9.4 %all_to_all.85 = f32[8,1,2048]{2,1,0:T(1,128)S(1)} all-to-all(f32[8,1,2048]{2,1,0:T(1,128)S(1)} %bitcast.34), channel_id=1, replica_groups=mesh['far'=8,'near'=2,'dom'=8,'coef'=4] {'dom'}, dimensions={0} | all-to-all | bytes 131072 | tf_op jit(solution)/shard_map/all_to_all | solution.py:261
  51.3 0.9 fwd0.1
  52.3 8.6 %all_to_all.86 = f32[4,1,5120]{2,1,0:T(1,128)S(1)} all-to-all(f32[4,1,5120]{2,1,0:T(1,128)S(1)} %bitcast.40), channel_id=1, replica_groups=mesh['far'=8,'near'=2,'dom'=8,'coef'=4] {'coef'}, dimensions={0} | all-to-all | bytes 163840 | tf_op jit(solution)/shard_map/all_to_all | solution.py:261
  60.8 1.5 %back1.1 = (f32[128,128]{1,0:T(8,128)S(1)}, f32[32,128]{1,0:T(8,128)S(1)}, f32[8,128]{1,0:T(8,128)S(1)}) custom-call(f32[8,4096]{1,0:T(8,128)S(1)} %get-tuple-element.24.geom, f32[8,4096]{1,0:T(8,128)S(1)} %get-tuple-element.30.high, bf16[96,256]{1,0:T(8,128)(2,1)S(1)} %get-tuple-element.31.picks, bf16[256,256]{1,0:T(8,128)(2,1)S(1)} %get-tuple-element.32.spread, ...), custom_call_target="tpu_custom_call" | custom-call | tf_op jit(solution)/shard_map/back1/pallas_call | solution.py:31
  62.4 10.8 %all_to_all.87 = f32[16,1,1024]{2,1,0:T(1,128)S(1)} all-to-all(f32[16,1,1024]{2,1,0:T(1,128)S(1)} %bitcast.42), channel_id=1, replica_groups=mesh['far'=8,'near'=2,'dom'=8,'coef'=4] {'dom','near'}, dimensions={0} | all-to-all | bytes 131072 | tf_op jit(solution)/shard_map/all_to_all | solution.py:261
  73.2 14.5 %all_to_all.88 = f32[16,1,1024]{2,1,0:T(1,128)S(1)} all-to-all(f32[16,1,1024]{2,1,0:T(1,128)S(1)} %bitcast.36), channel_id=1, replica_groups=mesh['far'=8,'near'=2,'dom'=8,'coef'=4] {'far','near'}, dimensions={0} | all-to-all | bytes 131072 | tf_op jit(solution)/shard_map/all_to_all | solution.py:261
  87.7 9.4 %all_to_all.89 = f32[8,1,2048]{2,1,0:T(1,128)S(1)} all-to-all(f32[8,1,2048]{2,1,0:T(1,128)S(1)} %bitcast.38), channel_id=1, replica_groups=mesh['far'=8,'near'=2,'dom'=8,'coef'=4] {'dom'}, dimensions={0} | all-to-all | bytes 131072 | tf_op jit(solution)/shard_map/all_to_all | solution.py:261
  97.1 0.9 fwd1.1
  98.0 6.9 %all_to_all.90 = f32[4,1,5120]{2,1,0:T(1,128)S(1)} all-to-all(f32[4,1,5120]{2,1,0:T(1,128)S(1)} %bitcast.39), channel_id=1, replica_groups=mesh['far'=8,'near'=2,'dom'=8,'coef'=4] {'coef'}, dimensions={0} | all-to-all | bytes 163840 | tf_op jit(solution)/shard_map/all_to_all | solution.py:261
  104.9 0.1 norm.1
  105.0 21.6 %all_to_all.91 = f32[128,1,128]{2,1,0:T(1,128)S(1)} all-to-all(f32[128,1,128]{2,1,0:T(1,128)S(1)} %bitcast.43), channel_id=1, replica_groups=mesh['far'=8,'near'=2,'dom'=8,'coef'=4] {'far','near','dom'}, dimensions={0} | all-to-all | bytes 131072 | tf_op jit(solution)/shard_map/all_to_all | solution.py:261
  126.6 0.8 last.1
  (4 shorter events, 0.1 us)
